TPU v7x, 32 devices: a whole 2x2x4 slice. The times are simulated.
32 devices in a mesh: ens: 2 (over y), space: 4 (over z), tm: 2 (over x), spin: 2 (over core).
Axes of the slice: x: 2, y: 2, z: 4, core: 2. Of those that a mesh axis runs over, the one named last changes fastest.
Arguments:
- eigvecs: bfloat16 [4, 2, 3, 8192, 128], P('tm', None, None, 'space'), may hold values from -6 to 6
- links: bfloat16 [4, 3, 2, 3, 3, 8192], P('tm', None, None, None, None, 'space'), may hold values from -2.5 to 2.5
- directions: int32 [4], P('spin'), may hold values from 0 to 3, each once
- pair_list: int32 [32, 2], P(('space', 'tm')), may hold values from 0 to 3
- pair_operators: int32 [32, 2], P(('space', 'tm')), may hold values from 0 to 3
- perambulators: bfloat16 [32, 16, 2, 128, 128], P(('space', 'tm'), 'spin'), may hold values from -0.5 to 0.5
Outputs:
- elementals: float32 [8, 4, 128, 2, 128], P(('ens', 'tm'), 'spin', 'space'), parts along dimension 0
- correlators: float32 [64, 2], P(('ens', 'space', 'tm')), parts along dimension 0
There are 2 independent parts, one for each index of `ens`. A program takes and returns all parts, laid end to end along the dimension named above; an argument that names none is the same for every part. Nothing has to cross between parts.
Inputs may be any that keep to these rules, and one draw needn't show every extreme that they name: `directions`: each code once; 0, 1, 2 name a covariant derivative along the first, second and third spatial direction, 3 the eigenvectors with one unit of momentum along the third.
All inputs are finite; a program needn't handle non-finite values.
Results may differ from a plain program's by a relative error of at most 0.0071.
Values may be sent and summed in bfloat16 or wider, within the bound.
A program may use at most 128 MiB of HBM per device.

v0:
```python
from functools import partial
import math

import jax
import jax.numpy as jnp
from jax import lax
from jax.sharding import PartitionSpec as P

PX = 16
PY = 16


def from_behind(array, axis, by):
    count = lax.axis_size(axis)
    return lax.ppermute(array, axis, [(i, (i + by) % count) for i in range(count)])


def apply_links(link_field, vectors):
    for b in range(3):
        link_real = link_field[0, :, b][..., None]
        link_imag = link_field[1, :, b][..., None]
        term_real = link_real * vectors[0, b] - link_imag * vectors[1, b]
        term_imag = link_real * vectors[1, b] + link_imag * vectors[0, b]
        if b == 0:
            total_real, total_imag = (term_real, term_imag)
        else:
            total_real, total_imag = (total_real + term_real, total_imag + term_imag)
    return jnp.stack([total_real, total_imag])


def apply_adjoint(link_field, vectors):
    for b in range(3):
        link_real = link_field[0, b][..., None]
        link_imag = link_field[1, b][..., None]
        term_real = link_real * vectors[0, b] + link_imag * vectors[1, b]
        term_imag = link_real * vectors[1, b] - link_imag * vectors[0, b]
        if b == 0:
            total_real, total_imag = (term_real, term_imag)
        else:
            total_real, total_imag = (total_real + term_real, total_imag + term_imag)
    return jnp.stack([total_real, total_imag])


def phase_field(vectors, z_coord, z_total):
    angles = 2.0 * math.pi / z_total * z_coord
    cosine_part = jnp.cos(angles)[:, None, None, None]
    sine_part = jnp.sin(angles)[:, None, None, None]
    return jnp.stack(
        [
            cosine_part * vectors[0] + sine_part * vectors[1],
            cosine_part * vectors[1] - sine_part * vectors[0],
        ]
    )


def covariant(direction, vectors, link_field, upper_rim, lower_rim):
    roll_axis = 4 - direction
    links_along = link_field[direction]
    forward = apply_links(links_along, jnp.roll(vectors, -1, roll_axis))
    backward = jnp.roll(apply_adjoint(links_along, vectors), 1, roll_axis)
    return 0.5 * (forward - backward)


def covariant_third(vectors, link_field, upper_rim, lower_rim):
    links_along = link_field[2]
    forward = apply_links(links_along, jnp.concatenate([vectors[:, :, 1:], upper_rim], axis=2))
    inner = apply_adjoint(links_along[:, :, :, :-1], vectors[:, :, :-1])
    backward = jnp.concatenate([lower_rim, inner], axis=2)
    return 0.5 * (forward - backward)


def gram_block(vectors_half, displaced, scaling):
    columns = vectors_half.shape[-1]
    left_side = vectors_half.reshape(-1, columns)
    displaced_half = displaced.astype(jnp.bfloat16)
    field_real = displaced_half[0].reshape(-1, columns)
    field_imag = displaced_half[1].reshape(-1, columns)
    right_side = jnp.concatenate(
        [
            jnp.concatenate([field_real, field_imag], 0),
            jnp.concatenate([field_imag, -field_real], 0),
        ],
        1,
    )
    product = lax.dot_general(
        left_side, right_side, (((0,), (0,)), ((), ())), preferred_element_type=jnp.float32
    )
    return (product * scaling).reshape(columns, 2, columns)


def contract_pair(source, sink_matrix, blocks, pair_signs):
    columns = source.shape[-1]
    sink_block = jnp.concatenate(
        [
            jnp.concatenate([sink_matrix[:, 0], -sink_matrix[:, 1]], 1),
            jnp.concatenate([sink_matrix[:, 1], sink_matrix[:, 0]], 1),
        ],
        0,
    )
    source_block = jnp.concatenate(
        [
            jnp.concatenate([source[:, 0], source[:, 1]], 1),
            jnp.concatenate([-source[:, 1], source[:, 0]], 1),
        ],
        0,
    )
    source_block = source_block.reshape(2, columns, 2 * columns)
    stacked = blocks.reshape(blocks.shape[0], 2 * columns, columns)
    halfway = jnp.einsum(
        "mk,qkn->qmn", sink_block, stacked, preferred_element_type=jnp.float32
    ).astype(jnp.bfloat16)
    second = jnp.einsum(
        "qcmk,ckn->qmn",
        halfway.reshape(-1, 2, columns, columns),
        source_block,
        preferred_element_type=jnp.float32,
    )
    tau_real = blocks[:, 0].astype(jnp.float32)
    tau_imag = blocks[:, 1].astype(jnp.float32)
    out_real = second[:, :, :columns]
    out_imag = second[:, :, columns:]
    trace_real = jnp.sum(out_real * tau_real + out_imag * tau_imag, axis=(1, 2))
    trace_imag = jnp.sum(out_imag * tau_real - out_real * tau_imag, axis=(1, 2))
    return jnp.stack([jnp.sum(pair_signs * trace_real), jnp.sum(pair_signs * trace_imag)]) / (
        4.0 * columns
    )


def shards(eigvecs, links, directions, pair_list, pair_operators, perambulators):
    slices = eigvecs.shape[0]
    local_sites = eigvecs.shape[3]
    columns = eigvecs.shape[4]
    plane_sites = PX * PY
    plane_count = local_sites // plane_sites
    layers = lax.axis_size("space")
    z_total = plane_count * layers
    scaling = 1.0 / math.sqrt(6.0 * plane_sites * z_total)
    z_coord = (lax.axis_index("space") * plane_count + jnp.arange(plane_count)).astype(jnp.float32)
    plane_above = from_behind(eigvecs[:, :, :, :plane_sites], "space", -1)
    top_vectors = eigvecs[:, :, :, local_sites - plane_sites :]
    top_links = links[:, 2, :, :, :, local_sites - plane_sites :]
    moved_vectors = from_behind(top_vectors, "space", 1)
    moved_links = from_behind(top_links, "space", 1)
    plane_below = jax.vmap(apply_adjoint)(
        moved_links.astype(jnp.float32), moved_vectors.astype(jnp.float32)
    )
    branches = [
        partial(covariant, 0),
        partial(covariant, 1),
        covariant_third,
        lambda vectors, link_field, upper_rim, lower_rim: phase_field(vectors, z_coord, z_total),
    ]
    op_slots = directions.shape[0]

    def per_slice(inputs):
        vectors_half, link_half, above_half, below_slice = inputs
        vectors = vectors_half.astype(jnp.float32).reshape(2, 3, plane_count, PY, PX, columns)
        link_field = link_half.astype(jnp.float32).reshape(3, 2, 3, 3, plane_count, PY, PX)
        upper_rim = above_half.astype(jnp.float32).reshape(2, 3, 1, PY, PX, columns)
        lower_rim = below_slice.reshape(2, 3, 1, PY, PX, columns)
        blocks = []
        for op_slot in range(op_slots):
            displaced = lax.switch(
                directions[op_slot], branches, vectors, link_field, upper_rim, lower_rim
            )
            blocks.append(gram_block(vectors_half, displaced, scaling))
        return jnp.stack(blocks)

    partials = lax.map(per_slice, (eigvecs, links, plane_above, plane_below))
    spin_size = lax.axis_size("spin")
    totals = lax.psum(partials, "space")
    row_count = columns // layers
    elementals = lax.dynamic_slice_in_dim(totals, lax.axis_index("space") * row_count, row_count, 2)
    elemental_table = lax.all_gather(
        totals.astype(jnp.bfloat16)[None], ("tm", "spin"), axis=0, tiled=True
    )
    flattened = elemental_table.reshape(-1, columns, 2, columns)
    position = (
        (pair_list // slices * spin_size + pair_operators // op_slots) * slices + pair_list % slices
    ) * op_slots + pair_operators % op_slots
    source_rows = flattened[position[:, 0]]
    sink_rows = flattened[position[:, 1]]
    pair_count = perambulators.shape[1]
    spin_pair = lax.axis_index("spin") * pair_count + jnp.arange(pair_count)
    first_sign = jnp.where(spin_pair // 4 < 2, 1.0, -1.0)
    later_sign = jnp.where(spin_pair % 4 < 2, 1.0, -1.0)
    pair_signs = (first_sign * later_sign).astype(jnp.float32)

    def per_pair(inputs):
        source, sink_matrix, blocks = inputs
        return contract_pair(source, sink_matrix, blocks, pair_signs)

    partial_corr = lax.map(per_pair, (source_rows, sink_rows, perambulators))
    correlators = lax.psum(partial_corr, "spin")
    return (elementals, correlators)


def solution(mesh):
    return jax.shard_map(
        shards,
        mesh=mesh,
        in_specs=(
            P("tm", None, None, "space", None),
            P("tm", None, None, None, None, "space"),
            P("spin"),
            P(("space", "tm"), None),
            P(("space", "tm"), None),
            P(("space", "tm"), "spin", None, None, None),
        ),
        out_specs=(P(("ens", "tm"), "spin", "space", None, None), P(("ens", "space", "tm"), None)),
        check_vma=False,
    )
```

profile of v0, /device:TPU:0, one launch (start us, length us, event | category | flops | bytes accessed | tf_op | source)
XLA Modules:
  0.0 290.6 jit_solution(11844642984709961674)
XLA Ops:
  8.0 3.1 %collective-permute-start.1 = (bf16[2,2,3,3,256]{4,1,3,2,0:T(2,128)(2,1)S(1)}, bf16[2,2,3,3,256]{4,1,3,2,0:T(2,128)(2,1)S(1)}, u32[]{:S(2)}, u32[]{:S(2)}) collective-permute-start(bf16[2,2,3,3,256]{4,1,3,2,0:T(2,128)(2,1)S(1)} %slice_bitcast_fusion.126), channel_id=1, source_target_pairs={{0,4},{4,8},{8,12},{12,0},{1,5},{5,9},{9,13},{13,1},{2,6},{6,10},{... | collective-permute-start | bytes 55304 | tf_op jit(solution)/shard_map/ppermute | solution.py:15
  11.1 2.4 fusion.140
  13.5 1.6 collective-permute-start.2
  15.1 2.2 collective-permute-start
  19.4 16.4 %collective-permute-done.2 = bf16[2,2,3,256,128]{4,3,2,1,0:T(8,128)(2,1)S(1)} collective-permute-done((bf16[2,2,3,256,128]{4,3,2,1,0:T(8,128)(2,1)S(1)}, bf16[2,2,3,256,128]{4,3,2,1,0:T(8,128)(2,1)S(1)}, u32[]{:S(2)}, u32[]{:S(2)}) %collective-permute-start.2) | collective-permute-done | bytes 786464 | tf_op jit(solution)/shard_map/ppermute | solution.py:15
  36.0 1.4 add_add_fusion.12
  38.7 12.3 %collective-permute-done = bf16[2,2,3,256,128]{4,3,2,1,0:T(8,128)(2,1)} collective-permute-done((bf16[2,2,3,256,128]{4,3,2,1,0:T(8,128)(2,1)}, bf16[2,2,3,256,128]{4,3,2,1,0:T(8,128)(2,1)}, u32[]{:S(2)}, u32[]{:S(2)}) %collective-permute-start) | collective-permute-done | bytes 786464 | tf_op jit(solution)/shard_map/ppermute | solution.py:15
  51.0 113.6 %while.24 = (s32[]{:T(128)}, f32[2,2,128,2,128]{4,2,3,1,0:T(8,128)}, bf16[2,2,3,2048,128]{4,3,2,1,0:T(8,128)(2,1)}, bf16[2,3,2,3,3,2048]{5,2,4,3,1,0:T(2,128)(2,...) while((s32[]{:T(128)}, ...), condition=%wide.region_9.10_spmd.clone, body=%wide.region_0.9_spmd.clone.sunk | while | flops 1758900224 | bytes 315630656 | solution.py:169
  51.0 2.1 constant_dynamic-slice_fusion.11
  53.1 3.7 %convert.50 = f32[2,3,8,16,16,128]{5,4,3,2,1,0:T(8,128)} convert(bf16[2,3,8,16,16,128]{5,4,3,2,1,0:T(8,128)(2,1)S(1)} %bitcast.469) | non-fusion elementwise | flops 1572864 | bytes 9437184 | tf_op jit(solution)/shard_map/while/body/eval_jaxpr/convert_element_type | solution.py:157
  57.9 2.3 reshape.1168
  61.3 1.5 constant_dynamic-slice_fusion.13
  63.7 10.0 %conditional.7 = (bf16[6144,128]{1,0:T(8,128)(2,1)S(1)}, bf16[6144,128]{1,0:T(8,128)(2,1)S(1)}) conditional(s32[]{:T(128)} %get-tuple-element.872, (f32[3,2,3,3,8,16,16]{6,5,4,1,3,2,0:T(8,128)S(1)}, f32[2,3,8,16,16,128]{5,4,3,2,1,0:T(8,128)}) %tuple.370, (f32[3,2,3,3,8,16,16]{6,5,4,1,3,2,0:T(8,128)S(1)}, ...), branch_computations={%region_1.1_spmd, %region_2.2_spmd, %region_3.3_spmd, %region_4.4_... | conditional | flops 47185920 | bytes 112312368 | solution.py:163
  69.9 3.8 %subtract_convert_fusion = (bf16[1,3,8,16,16,128]{5,4,3,2,1,0:T(8,128)(2,1)S(1)}, bf16[1,3,8,16,16,128]{5,4,3,2,1,0:T(8,128)(2,1)S(1)}) fusion(f32[2,3,8,16,16,128]{5,4,3,2,1,0:T(8,128)} %get-tuple-element.319, f32[8]{0:T(128)S(1)} %get-tuple-element.585, f32[8]{0:T(128)S(1)} %get-tuple-element.584), kind=kLoop, calls=%fused_computation.154 | loop fusion | flops 6291456 | bytes 9437248 | tf_op jit(solution)/shard_map/convert.3
  74.1 1.6 copy-done.5
  75.6 1.8 fusion.172
  77.5 1.6 reshape.1170
  79.1 23.6 %conditional.6 = (bf16[6144,128]{1,0:T(8,128)(2,1)S(1)}, bf16[6144,128]{1,0:T(8,128)(2,1)S(1)}) conditional(s32[]{:T(128)} %get-tuple-element.873, (f32[3,2,3,3,8,16,16]{6,5,4,1,3,2,0:T(8,128)S(1)}, f32[2,3,8,16,16,128]{5,4,3,2,1,0:T(8,128)}) %tuple.370, (f32[3,2,3,3,8,16,16]{6,5,4,1,3,2,0:T(8,128)S(1)}, ...), branch_computations={%region_5.5_spmd, %region_6.6_spmd, %region_7.7_spmd, %region_8.8_... | conditional | flops 47185920 | bytes 112312368 | solution.py:163
  85.4 3.0 %slice_bitcast_fusion.101 = (f32[7,16,16,128]{3,2,1,0:T(8,128)S(1)}, f32[7,16,16,128]{3,2,1,0:T(8,128)S(1)}, f32[7,16,16,128]{3,2,1,0:T(8,128)S(1)}, f32[7,16,16...) fusion(f32[2,3,8,16,16,128]{5,4,3,2,1,0:T(8,128)} %get-tuple-element.325), kind=kLoop, calls=%fused_computation.295 | loop fusion | bytes 11010048 | tf_op jit(solution)/shard_map/while/body/eval_jaxpr/cond/branch_2_fun/mul | solution.py:35
  88.6 4.4 %add_add_fusion.11 = (f32[1,3,7,16,16,128]{5,4,3,2,1,0:T(8,128)S(1)}, f32[1,3,7,16,16,128]{5,4,3,2,1,0:T(8,128)S(1)}) fusion(f32[7,16,16,128]{3,2,1,0:T(8,128)S(1)} %get-tuple-element.655, f32[3,7,16,16]{3,2,1,0:T(8,128)S(1)} %get-tuple-element.665, f32[7,16,16,128]{3,2,1,0:T(8,128)S(1)} %get-tuple-element.651, f32[3,7,16,16]{3,2,1,0:T(8,128)S(1)} %get-tuple-element.666, ...), kind=kLoop, calls=%fused_computation.276 | loop fusion | flops 15138816 | bytes 11139072 | tf_op jit(solution)/shard_map/while/body/eval_jaxpr/cond/branch_2_fun/add | solution.py:40
  95.1 5.2 %subtract_add_fusion.10 = (f32[1,3,8,16,16,128]{5,4,3,2,1,0:T(8,128)S(1)}, f32[1,3,8,16,16,128]{5,4,3,2,1,0:T(8,128)S(1)}) fusion(f32[8,16,16,128]{3,2,1,0:T(8,128)S(1)} %get-tuple-element.660, f32[3,8,16,16]{3,2,1,0:T(8,128)S(1)} %get-tuple-element.671, f32[8,16,16,128]{3,2,1,0:T(8,128)S(1)} %get-tuple-element.661, ...), kind=kLoop, calls=%fused_computation.274 | loop fusion | flops 17301504 | bytes 12730368 | tf_op jit(solution)/shard_map/while/body/eval_jaxpr/cond/branch_2_fun/add | solution.py:27
  100.3 1.4 fusion.78
  103.0 1.6 copy-done.6
  106.7 2.1 constant_dynamic-slice_fusion.11
  108.8 3.7 %convert.50 = f32[2,3,8,16,16,128]{5,4,3,2,1,0:T(8,128)} convert(bf16[2,3,8,16,16,128]{5,4,3,2,1,0:T(8,128)(2,1)S(1)} %bitcast.469) | non-fusion elementwise | flops 1572864 | bytes 9437184 | tf_op jit(solution)/shard_map/while/body/eval_jaxpr/convert_element_type | solution.py:157
  113.6 2.3 reshape.1168
  117.0 1.5 constant_dynamic-slice_fusion.13
  119.4 10.2 %conditional.7 = (bf16[6144,128]{1,0:T(8,128)(2,1)S(1)}, bf16[6144,128]{1,0:T(8,128)(2,1)S(1)}) conditional(s32[]{:T(128)} %get-tuple-element.872, (f32[3,2,3,3,8,16,16]{6,5,4,1,3,2,0:T(8,128)S(1)}, f32[2,3,8,16,16,128]{5,4,3,2,1,0:T(8,128)}) %tuple.370, (f32[3,2,3,3,8,16,16]{6,5,4,1,3,2,0:T(8,128)S(1)}, ...), branch_computations={%region_1.1_spmd, %region_2.2_spmd, %region_3.3_spmd, %region_4.4_... | conditional | flops 47185920 | bytes 112312368 | solution.py:163
  125.7 3.8 %subtract_convert_fusion = (bf16[1,3,8,16,16,128]{5,4,3,2,1,0:T(8,128)(2,1)S(1)}, bf16[1,3,8,16,16,128]{5,4,3,2,1,0:T(8,128)(2,1)S(1)}) fusion(f32[2,3,8,16,16,128]{5,4,3,2,1,0:T(8,128)} %get-tuple-element.319, f32[8]{0:T(128)S(1)} %get-tuple-element.585, f32[8]{0:T(128)S(1)} %get-tuple-element.584), kind=kLoop, calls=%fused_computation.154 | loop fusion | flops 6291456 | bytes 9437248 | tf_op jit(solution)/shard_map/convert.3
  129.8 1.6 copy-done.5
  131.4 1.8 fusion.172
  133.2 1.6 reshape.1170
  134.9 23.4 %conditional.6 = (bf16[6144,128]{1,0:T(8,128)(2,1)S(1)}, bf16[6144,128]{1,0:T(8,128)(2,1)S(1)}) conditional(s32[]{:T(128)} %get-tuple-element.873, (f32[3,2,3,3,8,16,16]{6,5,4,1,3,2,0:T(8,128)S(1)}, f32[2,3,8,16,16,128]{5,4,3,2,1,0:T(8,128)}) %tuple.370, (f32[3,2,3,3,8,16,16]{6,5,4,1,3,2,0:T(8,128)S(1)}, ...), branch_computations={%region_5.5_spmd, %region_6.6_spmd, %region_7.7_spmd, %region_8.8_... | conditional | flops 47185920 | bytes 112312368 | solution.py:163
  141.0 3.0 %slice_bitcast_fusion.101 = (f32[7,16,16,128]{3,2,1,0:T(8,128)S(1)}, f32[7,16,16,128]{3,2,1,0:T(8,128)S(1)}, f32[7,16,16,128]{3,2,1,0:T(8,128)S(1)}, f32[7,16,16...) fusion(f32[2,3,8,16,16,128]{5,4,3,2,1,0:T(8,128)} %get-tuple-element.325), kind=kLoop, calls=%fused_computation.295 | loop fusion | bytes 11010048 | tf_op jit(solution)/shard_map/while/body/eval_jaxpr/cond/branch_2_fun/mul | solution.py:35
  144.2 4.4 %add_add_fusion.11 = (f32[1,3,7,16,16,128]{5,4,3,2,1,0:T(8,128)S(1)}, f32[1,3,7,16,16,128]{5,4,3,2,1,0:T(8,128)S(1)}) fusion(f32[7,16,16,128]{3,2,1,0:T(8,128)S(1)} %get-tuple-element.655, f32[3,7,16,16]{3,2,1,0:T(8,128)S(1)} %get-tuple-element.665, f32[7,16,16,128]{3,2,1,0:T(8,128)S(1)} %get-tuple-element.651, f32[3,7,16,16]{3,2,1,0:T(8,128)S(1)} %get-tuple-element.666, ...), kind=kLoop, calls=%fused_computation.276 | loop fusion | flops 15138816 | bytes 11139072 | tf_op jit(solution)/shard_map/while/body/eval_jaxpr/cond/branch_2_fun/add | solution.py:40
  150.7 5.2 %subtract_add_fusion.10 = (f32[1,3,8,16,16,128]{5,4,3,2,1,0:T(8,128)S(1)}, f32[1,3,8,16,16,128]{5,4,3,2,1,0:T(8,128)S(1)}) fusion(f32[8,16,16,128]{3,2,1,0:T(8,128)S(1)} %get-tuple-element.660, f32[3,8,16,16]{3,2,1,0:T(8,128)S(1)} %get-tuple-element.671, f32[8,16,16,128]{3,2,1,0:T(8,128)S(1)} %get-tuple-element.661, ...), kind=kLoop, calls=%fused_computation.274 | loop fusion | flops 17301504 | bytes 12730368 | tf_op jit(solution)/shard_map/while/body/eval_jaxpr/cond/branch_2_fun/add | solution.py:27
  155.9 1.4 fusion.78
  158.6 1.6 copy-done.6
  164.7 68.7 %all-reduce.2.cloned.1.call-done = f32[2,2,128,2,128]{4,2,3,1,0:T(8,128)} async-done(((f32[2,2,128,2,128]{4,2,3,1,0:T(8,128)}), f32[2,2,128,2,128]{4,2,3,1,0:T(8,128)}) %all-reduce.2.cloned.1.call-update) | async-done | bytes 524304 | tf_op jit(solution)/shard_map/psum | solution.py:171
  233.4 1.8 convert_element_type.114
  237.0 14.9 %all-gather.3.cloned.1.call-done = bf16[8,2,128,2,128]{4,2,3,1,0:T(8,128)(2,1)} async-done(((bf16[2,2,128,2,128]{4,2,3,1,0:T(8,128)(2,1)}), bf16[8,2,128,2,128]{4,2,3,1,0:T(8,128)(2,1)}) %all-gather.3.cloned.1.call-update) | async-done | bytes 1048592 | tf_op jit(solution)/shard_map/all_gather | solution.py:174
  251.8 1.8 gather_fusion
  253.7 1.8 gather_fusion.1
  255.5 25.0 %while.25 = (s32[]{:T(128)}, f32[4,2]{0,1:T(2,128)S(1)}, bf16[4,8,2,128,128]{4,3,2,1,0:T(8,128)(2,1)}, bf16[4,128,2,128]{3,1,2,0:T(8,128)(2,1)S(1)}, bf16[4,128,...) while((s32[]{:T(128)}, f32[4,2]{0,1:T(2,128)S(1)}, ...), condition=%wide.region_16.17_spmd.clone, body=%wide.region_11.16_spmd.clone.sunk | while | flops 271090112 | bytes 8454929 | solution.py:193
  260.4 1.3 maximum_multiply_fusion.2
  266.6 1.3 maximum_multiply_fusion.2
  272.8 1.3 maximum_multiply_fusion.2
  280.5 3.0 %psum.15 = f32[4,2]{0,1:T(2,128)} all-reduce(f32[4,2]{0,1:T(2,128)S(1)} %get-tuple-element.356), channel_id=1, replica_groups=mesh['ens'=2,'space'=4,'tm'=2,'spin'=2] {'spin'}, use_global_device_ids=true, to_apply=%region_17.18 | all-reduce | flops 8 | bytes 64 | tf_op jit(solution)/shard_map/psum | solution.py:194
  (170 shorter events, 43.2 us)
Async XLA Ops:
  7.2 10.2 %copy-start.13 = (s32[2]{0:T(128)S(1)}, s32[2]{0:T(128)}, u32[]{:S(2)}) copy-start(s32[2]{0:T(128)} %param.20) | copy-start | bytes 28
  7.2 226.2 %all-reduce.2.cloned.1.call-start = ((), (), s32[]{:S(2)}) async-start(), calls=%async_computation | async-start | bytes 1048576 | tf_op jit(solution)/shard_map/psum | solution.py:171
  8.0 11.3 %collective-permute-start.1 = (bf16[2,2,3,3,256]{4,1,3,2,0:T(2,128)(2,1)S(1)}, bf16[2,2,3,3,256]{4,1,3,2,0:T(2,128)(2,1)S(1)}, u32[]{:S(2)}, u32[]{:S(2)}) collective-permute-start(bf16[2,2,3,3,256]{4,1,3,2,0:T(2,128)(2,1)S(1)} %slice_bitcast_fusion.126), channel_id=1, source_target_pairs={{0,4},{4,8},{8,12},{12,0},{1,5},{5,9},{9,13},{13,1},{2,6},{6,10},{... | collective-permute-start | bytes 55304 | tf_op jit(solution)/shard_map/ppermute | solution.py:15
  13.5 22.3 %collective-permute-start.2 = (bf16[2,2,3,256,128]{4,3,2,1,0:T(8,128)(2,1)S(1)}, bf16[2,2,3,256,128]{4,3,2,1,0:T(8,128)(2,1)S(1)}, u32[]{:S(2)}, u32[]{:S(2)}) collective-permute-start(bf16[2,2,3,256,128]{4,3,2,1,0:T(8,128)(2,1)S(1)} %get-tuple-element.686), channel_id=1, source_target_pairs={{0,4},{4,8},{8,12},{12,0},{1,5},{5,9},{9,13},{13,1},{2,6},{6,10},{... | collective-permute-start | bytes 2359304 | tf_op jit(solution)/shard_map/ppermute | solution.py:15
  15.1 35.9 %collective-permute-start = (bf16[2,2,3,256,128]{4,3,2,1,0:T(8,128)(2,1)}, bf16[2,2,3,256,128]{4,3,2,1,0:T(8,128)(2,1)}, u32[]{:S(2)}, u32[]{:S(2)}) collective-permute-start(bf16[2,2,3,256,128]{4,3,2,1,0:T(8,128)(2,1)} %get-tuple-element.687), channel_id=1, source_target_pairs={{0,12},{4,0},{8,4},{12,8},{1,13},{5,1},{9,5},{13,9},{2,14},{6,2},{... | collective-permute-start | bytes 2359304 | tf_op jit(solution)/shard_map/ppermute | solution.py:15
  51.0 184.2 %copy-start.14 = (s32[4,2]{0,1:T(2,128)S(1)}, s32[4,2]{0,1:T(2,128)}, u32[]{:S(2)}) copy-start(s32[4,2]{0,1:T(2,128)} %param.22) | copy-start | bytes 100
  51.0 184.2 %copy-start.15 = (s32[4,2]{0,1:T(2,128)S(1)}, s32[4,2]{0,1:T(2,128)}, u32[]{:S(2)}) copy-start(s32[4,2]{0,1:T(2,128)} %param.21) | copy-start | bytes 100
  53.1 3.7 %copy-start.4 = (bf16[1,2,3,2048,128]{4,3,2,1,0:T(8,128)(2,1)}, bf16[1,2,3,2048,128]{4,3,2,1,0:T(8,128)(2,1)S(1)}, u32[]{:S(2)}) copy-start(bf16[1,2,3,2048,128]{4,3,2,1,0:T(8,128)(2,1)S(1)} %constant_dynamic-slice_fusion.11) | copy-start | bytes 9437188 | tf_op jit(solution)/shard_map/while
  53.1 3.7 %copy-start.12 = (bf16[2,3,2,3,3,2048]{5,2,4,3,1,0:T(2,128)(2,1)S(1)}, bf16[2,3,2,3,3,2048]{5,2,4,3,1,0:T(2,128)(2,1)}, u32[]{:S(2)}) copy-start(bf16[2,3,2,3,3,2048]{5,2,4,3,1,0:T(2,128)(2,1)} %get-tuple-element.869) | copy-start | bytes 1327108 | tf_op jit(solution)/shard_map/while
  61.3 1.5 copy-start.7
  62.8 0.9 copy-start.9
  73.7 1.9 copy-start.5
  88.6 4.5 %slice-start.2 = ((s8[6291456]{0:T(1024)(128)(4,1)}), s8[4194304]{0:T(1024)(128)(4,1)S(1)}, s32[]{:S(2)}) async-start(s8[6291456]{0:T(1024)(128)(4,1)} %bitcast.467), calls=%async_computation.4 | async-start | bytes 8388608 | tf_op jit(solution)/shard_map/while/body/eval_jaxpr/cond
  88.6 4.5 %slice-start.3 = ((s8[6291456]{0:T(1024)(128)(4,1)}), s8[2097152]{0:T(1024)(128)(4,1)S(1)}, s32[]{:S(2)}) async-start(s8[6291456]{0:T(1024)(128)(4,1)} %bitcast.467), calls=%async_computation.5 | async-start | bytes 4194304 | tf_op jit(solution)/shard_map/while/body/eval_jaxpr/cond
  93.1 1.1 copy-start.8
  95.0 5.2 %copy-start.10 = (f32[2,3,1,16,16,128]{5,4,3,2,1,0:T(8,128)S(1)}, f32[2,3,1,16,16,128]{5,4,3,2,1,0:T(8,128)}, u32[]{:S(2)}) copy-start(f32[2,3,1,16,16,128]{5,4,3,2,1,0:T(8,128)} %get-tuple-element.327) | copy-start | bytes 2359300 | tf_op jit(solution)/shard_map/while/body/eval_jaxpr/cond
  102.7 1.9 copy-start.6
  104.6 1.3 copy-start.11
  108.8 3.7 %copy-start.4 = (bf16[1,2,3,2048,128]{4,3,2,1,0:T(8,128)(2,1)}, bf16[1,2,3,2048,128]{4,3,2,1,0:T(8,128)(2,1)S(1)}, u32[]{:S(2)}) copy-start(bf16[1,2,3,2048,128]{4,3,2,1,0:T(8,128)(2,1)S(1)} %constant_dynamic-slice_fusion.11) | copy-start | bytes 9437188 | tf_op jit(solution)/shard_map/while
  108.8 3.7 %copy-start.12 = (bf16[2,3,2,3,3,2048]{5,2,4,3,1,0:T(2,128)(2,1)S(1)}, bf16[2,3,2,3,3,2048]{5,2,4,3,1,0:T(2,128)(2,1)}, u32[]{:S(2)}) copy-start(bf16[2,3,2,3,3,2048]{5,2,4,3,1,0:T(2,128)(2,1)} %get-tuple-element.869) | copy-start | bytes 1327108 | tf_op jit(solution)/shard_map/while
  117.0 1.5 copy-start.7
  118.5 0.9 copy-start.9
  129.5 1.9 copy-start.5
  144.2 4.5 %slice-start.2 = ((s8[6291456]{0:T(1024)(128)(4,1)}), s8[4194304]{0:T(1024)(128)(4,1)S(1)}, s32[]{:S(2)}) async-start(s8[6291456]{0:T(1024)(128)(4,1)} %bitcast.467), calls=%async_computation.4 | async-start | bytes 8388608 | tf_op jit(solution)/shard_map/while/body/eval_jaxpr/cond
  144.2 4.5 %slice-start.3 = ((s8[6291456]{0:T(1024)(128)(4,1)}), s8[2097152]{0:T(1024)(128)(4,1)S(1)}, s32[]{:S(2)}) async-start(s8[6291456]{0:T(1024)(128)(4,1)} %bitcast.467), calls=%async_computation.5 | async-start | bytes 4194304 | tf_op jit(solution)/shard_map/while/body/eval_jaxpr/cond
  148.7 1.1 copy-start.8
  150.7 5.2 %copy-start.10 = (f32[2,3,1,16,16,128]{5,4,3,2,1,0:T(8,128)S(1)}, f32[2,3,1,16,16,128]{5,4,3,2,1,0:T(8,128)}, u32[]{:S(2)}) copy-start(f32[2,3,1,16,16,128]{5,4,3,2,1,0:T(8,128)} %get-tuple-element.327) | copy-start | bytes 2359300 | tf_op jit(solution)/shard_map/while/body/eval_jaxpr/cond
  158.3 1.9 copy-start.6
  160.2 1.3 copy-start.11
  164.6 87.2 %all-gather.3.cloned.1.call-start = ((), (), s32[]{:S(2)}) async-start(), calls=%async_computation.1 | async-start | bytes 1310720 | tf_op jit(solution)/shard_map/all_gather | solution.py:174
Sparse Core Ops, SparseCore 0:
  164.7 68.5 all-reduce.1
  235.3 16.4 all-gather.2
where the time goes:
time: 290 us; the launch traced here: 291 us
  waiting for transfers between devices  112 us (39%)
  other arithmetic  58.8 us (20%)
  local copies, waits for them, and re-layouts  57 us (20%)
  loops' own time  28.2 us (10%)
  between operations  15.9 us (5%)
  matrix products  8.55 us (3%)
  starting transfers between devices  7.01 us (2%)
  blocking collectives  3.01 us (1%)
    psum x1, waiting for transfers between devices, shards(): totals = lax.psum(partials, 'space')  68.7 us
    ppermute x3, waiting for transfers between devices, from_behind(): lax.ppermute(array, axis, [(i, (i + by) % count) for i in range(count)])  28.7 us
    another operation x4, loops' own time, per_slice(): lax.switch(directions[op_slot], branches, vectors, link_field, upper_rim,...  25.2 us
    all_gather x1, waiting for transfers between devices, shards(): lax.all_gather(totals.astype(jnp.bfloat16)[None], ('tm', 'spin'), axis=0,...  14.9 us
    add x2, other arithmetic, apply_links(): total_real, total_imag = (total_real + term_real, total_imag + term_imag)  10.5 us
    add x3, other arithmetic, apply_adjoint(): total_real, total_imag = (total_real + term_real, total_imag + term_imag)  10.3 us
    dynamic_slice x6, local copies, waits for them, and re-layouts, shards(): partials = lax.map(per_slice, (eigvecs, links, plane_above, plane_below))  9.22 us
    while x28, local copies, waits for them, and re-layouts  8.02 us
  transfers between devices with their start and end apart: 5, of which 4 were waited for; matrix products, arithmetic and copies ran while one was open for 3% of the time, Pallas kernels for 0%

commit v1 on v0

v1 whole, which is shorter than its diff:
```python
import functools
import math

import jax
import jax.numpy as jnp
from jax import lax
from jax.experimental import pallas as pl
from jax.experimental.pallas import tpu as pltpu
from jax.sharding import PartitionSpec as P

PX = 16
PY = 16
PLANE = PX * PY
BF = jnp.bfloat16
F32 = jnp.float32


def neighbour_mask(group, shift_x):
    row = lax.broadcasted_iota(jnp.int32, (group, group), 0)
    col = lax.broadcasted_iota(jnp.int32, (group, group), 1)
    if shift_x:
        col = (col // PX) * PX + lax.rem(col + 1, PX)
    return jnp.where(row == col, 1.0, 0.0).astype(BF)


def carried(links_ref, lead, offset, group, mask, real, imag):
    columns = real[0].shape[-1]
    rows = []
    for b in range(3):
        parts = []
        for part in range(2):
            for a in range(3):
                row = links_ref[lead + (part, a, pl.ds(b, 1), pl.ds(offset, group))]
                parts.append(jnp.broadcast_to(row, (group, group)) * mask)
        rows.append(jnp.concatenate(parts, axis=1))
    matrix = jnp.concatenate(rows, axis=0)
    weights = jnp.concatenate(
        [jnp.concatenate([real[a], -imag[a]], axis=1) for a in range(3)]
        + [jnp.concatenate([imag[a], real[a]], axis=1) for a in range(3)],
        axis=0,
    )
    return jnp.dot(matrix, weights, preferred_element_type=F32).astype(BF)


def gram(left, right):
    return lax.dot_general(left, right, (((0,), (0,)), ((), ())), preferred_element_type=F32)


def antihermitian(product, columns, scaling):
    real = product[:columns, :columns] - product[columns:, columns:]
    imag = product[:columns, columns:] + product[columns:, :columns]
    return jnp.concatenate(
        [(0.5 * scaling) * (real - real.T), (0.5 * scaling) * (imag + imag.T)], axis=1
    )


def ones_where(condition):
    return jnp.where(condition, 1.0, 0.0).astype(BF)


def spread(row, mask):
    return jnp.broadcast_to(row, mask.shape) * mask


def stencil(forward, backward, mask_up, mask_down):
    def block(part, a, b):
        up = forward[part * 9 + a * 3 + b : part * 9 + a * 3 + b + 1]
        down = backward[part * 9 + b * 3 + a : part * 9 + b * 3 + a + 1]
        ahead = spread(up, mask_up) if mask_up is not None else None
        behind = spread(down if part else -down, mask_down) if mask_down is not None else None
        if ahead is None:
            return behind
        return ahead if behind is None else ahead + behind

    return jnp.concatenate(
        [
            jnp.concatenate([block(part, a, b) for part in range(2) for b in range(3)], axis=1)
            for a in range(3)
        ],
        axis=0,
    )


def local_kernel(
    plane_count, columns, scaling, dirs, phases, v_ref, links_ref, out_ref, flipped, moved
):
    code = dirs[pl.program_id(1)]
    group = PLANE // 2
    groups = plane_count * 2
    sites = plane_count * PLANE
    strip = group // plane_count

    @pl.when(pl.program_id(1) == 0)
    def _():
        def step(n, carry):
            start = pl.multiple_of(n * group, group)
            for part in range(2):
                for a in range(3):
                    flipped[
                        pl.ds(part * columns, columns),
                        pl.ds(pl.multiple_of(a * sites + start, group), group),
                    ] = v_ref[0, part, a, pl.ds(start, group), :].T
            return carry

        lax.fori_loop(0, groups, step, 0)

    def weights(rows):
        real = [rows(0, a) for a in range(3)]
        imag = [rows(1, a) for a in range(3)]
        return jnp.concatenate(
            [jnp.concatenate([real[a], imag[a]], axis=1) for a in range(3)]
            + [jnp.concatenate([-imag[a], real[a]], axis=1) for a in range(3)],
            axis=0,
        )

    row = lax.broadcasted_iota(jnp.int32, (group, group), 0)
    col = lax.broadcasted_iota(jnp.int32, (group, group), 1)

    def natural(start):
        return lambda part, a: v_ref[0, part, a, pl.ds(start, group), :]

    def keep(start, value):
        value = value.astype(BF)
        for a in range(3):
            moved[a, pl.ds(start, group), :] = value[a * group : (a + 1) * group]

    @pl.when(code == 0)
    def _():
        base = (col // PX) * PX
        within = col - base
        mask_up = ones_where(row == base + lax.rem(within + PX - 1, PX))
        mask_down = ones_where(row == base + lax.rem(within + 1, PX))
        lane = lax.broadcasted_iota(jnp.int32, (18, group), 1)

        def step(n, carry):
            start = pl.multiple_of(n * group, group)
            field = links_ref[0, 0, :, pl.ds(start, group)]
            ahead = jnp.where(
                lax.rem(lane, PX) == 0,
                pltpu.roll(field, group - PX + 1, 1),
                pltpu.roll(field, 1, 1),
            )
            matrix = stencil(ahead.astype(BF), field.astype(BF), mask_up, mask_down)
            keep(start, jnp.dot(matrix, weights(natural(start)), preferred_element_type=F32))
            return carry

        lax.fori_loop(0, groups, step, 0)

    @pl.when(code == 1)
    def _():
        mask_up = ones_where(row == col - PX)
        mask_down = ones_where(row == col + PX)
        edge_row = lax.broadcasted_iota(jnp.int32, (PX, group), 0)
        edge_col = lax.broadcasted_iota(jnp.int32, (PX, group), 1)
        edge_up = ones_where(edge_row == edge_col)
        edge_down = ones_where(edge_row == edge_col - (group - PX))

        def step(plane, carry):
            base = pl.multiple_of(plane * PLANE, PLANE)
            starts = [pl.multiple_of(base + half * group, group) for half in range(2)]
            fields = [links_ref[0, 0, :, pl.ds(start, group)] for start in starts]
            turned = [pltpu.roll(field, PX, 1).astype(BF) for field in fields]
            fields = [field.astype(BF) for field in fields]
            loaded = [weights(natural(start)) for start in starts]
            for half in range(2):
                far = 1 - half
                matrix = stencil(turned[half], fields[half], mask_up, mask_down)
                edge = jnp.concatenate(
                    [
                        stencil(turned[half], fields[far], None, edge_down),
                        stencil(turned[half], fields[far], edge_up, None),
                    ],
                    axis=0,
                )
                value = jnp.dot(matrix, loaded[half], preferred_element_type=F32)
                rim = jnp.dot(edge, loaded[far], preferred_element_type=F32)
                pieces = []
                for a in range(3):
                    low, high = a * group, (a + 1) * group
                    pieces += [
                        value[low : low + PX] + rim[a * PX : (a + 1) * PX],
                        value[low + PX : high - PX],
                        value[high - PX : high] + rim[(3 + a) * PX : (4 + a) * PX],
                    ]
                keep(starts[half], jnp.concatenate(pieces, axis=0))
            return carry

        lax.fori_loop(0, plane_count, step, 0)

    @pl.when(code == 2)
    def _():
        mask_up = ones_where(row == col - strip)
        mask_down = ones_where(row == col + strip)

        def step(n, carry):
            start = pl.multiple_of(n * group, group)
            field = links_ref[0, 0, :, pl.ds(start, group)]
            ahead = pltpu.roll(field, strip, 1)
            matrix = stencil(ahead.astype(BF), field.astype(BF), mask_up, mask_down)
            places = [
                pl.multiple_of(z * PLANE + n * strip, strip) for z in range(plane_count)
            ]
            loaded = weights(
                lambda part, a: jnp.concatenate(
                    [v_ref[0, part, a, pl.ds(place, strip), :] for place in places], axis=0
                )
            )
            value = jnp.dot(matrix, loaded, preferred_element_type=F32).astype(BF)
            for a in range(3):
                for z, place in enumerate(places):
                    low = a * group + z * strip
                    moved[a, pl.ds(place, strip), :] = value[low : low + strip]
            return carry

        lax.fori_loop(0, groups, step, 0)

    @pl.when(code == 3)
    def _():
        def step(plane, carry):
            base = pl.multiple_of(plane * PLANE, PLANE)
            cosine, sine = phases[0, plane], phases[1, plane]
            for a in range(3):
                real = v_ref[0, 0, a, pl.ds(base, PLANE), :].astype(F32)
                imag = v_ref[0, 1, a, pl.ds(base, PLANE), :].astype(F32)
                moved[a, pl.ds(base, PLANE), :] = jnp.concatenate(
                    [cosine * real + sine * imag, cosine * imag - sine * real], axis=1
                ).astype(BF)
            return carry

        lax.fori_loop(0, plane_count, step, 0)

    product = jnp.zeros((2 * columns, 2 * columns), F32)
    for a in range(3):
        product += jnp.dot(
            flipped[:, a * sites : (a + 1) * sites], moved[a], preferred_element_type=F32
        )
    scale = jnp.where(code == 3, scaling, 0.5 * scaling)
    out_ref[0, 0] = scale * jnp.concatenate(
        [
            product[:columns, :columns] + product[columns:, columns:],
            product[:columns, columns:] - product[columns:, :columns],
        ],
        axis=1,
    )


def boundary_kernel(columns, scaling, dirs, v_ref, links_ref, above_ref, part_ref, out_ref):
    op_slots = part_ref.shape[1]
    group = PLANE // 2
    for slot in range(op_slots):
        @pl.when(dirs[slot] != 2)
        def _(slot=slot):
            out_ref[0, slot] = part_ref[0, slot].astype(out_ref.dtype)

        @pl.when(dirs[slot] == 2)
        def _(slot=slot):
            mask = neighbour_mask(group, False)
            total = jnp.zeros((2 * columns, 2 * columns), F32)
            for half in range(2):
                own = [
                    [v_ref[0, p, a, pl.ds(half * group, group), :] for a in range(3)]
                    for p in range(2)
                ]
                moved = carried(links_ref, (0, 0), half * group, group, mask, *own)
                other = jnp.concatenate(
                    [
                        jnp.concatenate(
                            [
                                above_ref[0, p, a, pl.ds(half * group, group), :]
                                for p in range(2)
                            ],
                            axis=1,
                        )
                        for a in range(3)
                    ],
                    axis=0,
                )
                total += gram(moved, other)
            out_ref[0, slot] = (
                part_ref[0, slot] + antihermitian(total, columns, scaling)
            ).astype(out_ref.dtype)


def contract_kernel(columns, quarter, positions, signs, source_ref, sink_ref, tau_ref, out_ref):
    def whole(ref):
        value = ref[...].astype(F32)
        return value.reshape(columns, 2 * columns).astype(BF)

    source, sink = whole(source_ref), whole(sink_ref)
    count = tau_ref.shape[1]
    sr, si = sink[:, :columns], sink[:, columns:]
    sink_block = jnp.concatenate(
        [jnp.concatenate([sr, -si], axis=1), jnp.concatenate([si, sr], axis=1)], axis=0
    )
    rr, ri = source[:, :columns], source[:, columns:]
    source_block = jnp.concatenate(
        [jnp.concatenate([rr, ri], axis=1), jnp.concatenate([-ri, rr], axis=1)], axis=0
    )
    total_real = jnp.zeros((8, columns), F32)
    total_imag = jnp.zeros((8, columns), F32)
    for first in range(0, count, 2):
        some = range(first, min(first + 2, count))
        stacked = jnp.concatenate(
            [
                jnp.concatenate([tau_ref[0, q, 0], tau_ref[0, q, 1]], axis=0)
                for q in some
            ],
            axis=1,
        )
        halfway = jnp.dot(sink_block, stacked, preferred_element_type=F32).astype(BF)
        lines = jnp.concatenate(
            [
                jnp.concatenate(
                    [
                        halfway[:columns, n * columns : (n + 1) * columns],
                        halfway[columns:, n * columns : (n + 1) * columns],
                    ],
                    axis=1,
                )
                for n in range(len(some))
            ],
            axis=0,
        )
        second = jnp.dot(lines, source_block, preferred_element_type=F32)
        for n, q in enumerate(some):
            out_real = second[n * columns : (n + 1) * columns, :columns]
            out_imag = second[n * columns : (n + 1) * columns, columns:]
            tau_real = tau_ref[0, q, 0].astype(F32)
            tau_imag = tau_ref[0, q, 1].astype(F32)
            real = out_real * tau_real + out_imag * tau_imag
            imag = out_imag * tau_real - out_real * tau_imag
            total_real += signs[q] * jnp.sum(real.reshape(-1, 8, columns), axis=0)
            total_imag += signs[q] * jnp.sum(imag.reshape(-1, 8, columns), axis=0)
    out_ref[0, 0] = total_real
    out_ref[0, 1] = total_imag


def shift_over(array, axis, by):
    count = lax.axis_size(axis)
    return lax.ppermute(array, axis, [(i, (i + by) % count) for i in range(count)])


def halo(eigvecs):
    plane = eigvecs[:, :, :, :PLANE]
    if lax.axis_size("spin") != 2:
        return shift_over(plane, "space", -1)
    core = lax.axis_index("spin")
    mine = lax.dynamic_slice_in_dim(plane, core, 1, 1)
    mine = shift_over(mine, "space", -1)
    theirs = shift_over(mine, "spin", 1)
    return jnp.concatenate(
        [jnp.where(core == 0, mine, theirs), jnp.where(core == 0, theirs, mine)], axis=1
    )


def shards(eigvecs, links, directions, pair_list, pair_operators, perambulators):
    slices, _, _, local_sites, columns = eigvecs.shape
    plane_count = local_sites // PLANE
    layers = lax.axis_size("space")
    tm_size = lax.axis_size("tm")
    spin_size = lax.axis_size("spin")
    z_total = plane_count * layers
    scaling = 1.0 / math.sqrt(6.0 * PLANE * z_total)
    op_slots = directions.shape[0]
    z_coord = (lax.axis_index("space") * plane_count + jnp.arange(plane_count)).astype(F32)
    angles = 2.0 * math.pi / z_total * z_coord
    phases = jnp.stack([jnp.cos(angles), jnp.sin(angles)])
    above = halo(eigvecs)

    flat = links.astype(F32).reshape(slices, 3, 18, local_sites)
    strips = flat[:, 2].reshape(slices, 18, plane_count, -1, PLANE // 2 // plane_count)
    strips = jnp.swapaxes(strips, 2, 3).reshape(slices, 1, 18, local_sites)
    flat = jnp.concatenate([flat[:, :2], strips], axis=1)

    partial = pl.pallas_call(
        functools.partial(local_kernel, plane_count, columns, scaling),
        out_shape=jax.ShapeDtypeStruct((slices, op_slots, columns, 2 * columns), F32),
        grid_spec=pltpu.PrefetchScalarGridSpec(
            num_scalar_prefetch=2,
            grid=(slices, op_slots),
            in_specs=[
                pl.BlockSpec((1, 2, 3, local_sites, columns), lambda t, o, d, f: (t, 0, 0, 0, 0)),
                pl.BlockSpec(
                    (1, 1, 18, local_sites),
                    lambda t, o, d, f: (t, jnp.minimum(d[o], 2), 0, 0),
                ),
            ],
            out_specs=pl.BlockSpec((1, 1, columns, 2 * columns), lambda t, o, d, f: (t, o, 0, 0)),
            scratch_shapes=[
                pltpu.VMEM((2 * columns, 3 * local_sites), BF),
                pltpu.VMEM((3, local_sites, 2 * columns), BF),
            ],
        ),
        compiler_params=pltpu.CompilerParams(vmem_limit_bytes=48 << 20),
        cost_estimate=pl.CostEstimate(
            flops=13_000_000_000, bytes_accessed=eigvecs.size * 2, transcendentals=0
        ),
        name="local_gram",
    )(directions, phases, eigvecs, flat)

    last = plane_count - 1
    summed = pl.pallas_call(
        functools.partial(boundary_kernel, columns, scaling),
        out_shape=jax.ShapeDtypeStruct(partial.shape, F32),
        grid_spec=pltpu.PrefetchScalarGridSpec(
            num_scalar_prefetch=1,
            grid=(slices,),
            in_specs=[
                pl.BlockSpec((1, 2, 3, PLANE, columns), lambda t, d: (t, 0, 0, last, 0)),
                pl.BlockSpec((1, 1, 2, 3, 3, PLANE), lambda t, d: (t, 2, 0, 0, 0, last)),
                pl.BlockSpec((1, 2, 3, PLANE, columns), lambda t, d: (t, 0, 0, 0, 0)),
                pl.BlockSpec((1, op_slots, columns, 2 * columns), lambda t, d: (t, 0, 0, 0)),
            ],
            out_specs=pl.BlockSpec((1, op_slots, columns, 2 * columns), lambda t, d: (t, 0, 0, 0)),
        ),
        name="boundary",
    )(directions, eigvecs, links, above, partial)

    rows = columns // layers
    owned = lax.psum_scatter(summed, "space", scatter_dimension=2, tiled=True)
    elementals = owned.reshape(slices, op_slots, rows, 2, columns)
    table = lax.all_gather(owned.astype(BF), ("space", "tm", "spin"), axis=0)
    table = table.reshape(layers, tm_size * spin_size * slices * op_slots, rows, 2 * columns)

    position = (
        (pair_list // slices * spin_size + pair_operators // op_slots) * slices + pair_list % slices
    ) * op_slots + pair_operators % op_slots
    pair_count, count = perambulators.shape[0], perambulators.shape[1]
    spin_pair = lax.axis_index("spin") * count + jnp.arange(count)
    signs = jnp.where((spin_pair // 4 < 2) == (spin_pair % 4 < 2), 1.0, -1.0).astype(F32)
    block = (layers, 1, rows, 2 * columns)
    traces = pl.pallas_call(
        functools.partial(contract_kernel, columns, 4),
        out_shape=jax.ShapeDtypeStruct((pair_count, 2, 8, columns), F32),
        grid_spec=pltpu.PrefetchScalarGridSpec(
            num_scalar_prefetch=2,
            grid=(pair_count,),
            in_specs=[
                pl.BlockSpec(block, lambda p, pos, s: (0, pos[p, 0], 0, 0)),
                pl.BlockSpec(block, lambda p, pos, s: (0, pos[p, 1], 0, 0)),
                pl.BlockSpec((1, count, 2, columns, columns), lambda p, pos, s: (p, 0, 0, 0, 0)),
            ],
            out_specs=pl.BlockSpec((1, 2, 8, columns), lambda p, pos, s: (p, 0, 0, 0)),
        ),
        name="contract",
    )(position, signs, table, table, perambulators)
    part = jnp.sum(traces, axis=(2, 3)) / (4.0 * columns)
    if spin_size == 2:
        correlators = part + shift_over(part, "spin", 1)
    else:
        correlators = lax.psum(part, "spin")
    return (elementals, correlators)


def solution(mesh):
    return jax.shard_map(
        shards,
        mesh=mesh,
        in_specs=(
            P("tm", None, None, "space", None),
            P("tm", None, None, None, None, "space"),
            P("spin"),
            P(("space", "tm"), None),
            P(("space", "tm"), None),
            P(("space", "tm"), "spin", None, None, None),
        ),
        out_specs=(P(("ens", "tm"), "spin", "space", None, None), P(("ens", "space", "tm"), None)),
        check_vma=False,
    )
```

time: 290 us -> 141 us (0.49)
  waiting for transfers between devices: 112 us -> 57.6 us
  other arithmetic: 58.8 us -> 5.74 us
  Pallas kernels: 0 us -> 41.6 us
  local copies, waits for them, and re-layouts: 57 us -> 15.8 us
  loops' own time: 28.2 us -> 0 us
  matrix products: 8.55 us -> 0 us
  blocking collectives: 3.01 us -> 0 us
    psum x1 -> x0, waiting for transfers between devices: 68.7 us -> none  [shards(): totals = lax.psum(partials, 'space')]
    pallas_call x0 -> x3, Pallas kernels: none -> 41.6 us  [the longest x1 33.1 us: shards(): pl.pallas_call(functools.partial(local_kernel, plane_count, columns, scal...]
    another operation x6 -> x0, loops' own time: 28.2 us -> none  [the longest x4 25.2 us: per_slice(): lax.switch(directions[op_slot], branches, vectors, link_field, upper_rim,...]
    ppermute x3, waiting for transfers between devices: 28.7 us -> 0.94 us  [shift_over(): lax.ppermute(array, axis, [(i, (i + by) % count) for i in range(count)])]
    reduce_scatter x0 -> x1, waiting for transfers between devices: none -> 22.9 us  [shards(): owned = lax.psum_scatter(summed, 'space', scatter_dimension=2, tiled=True)]
    add x5 -> x1, other arithmetic: 20.7 us -> 0.01 us  [shards(): correlators = part + shift_over(part, 'spin', 1)]
    all_gather x1, waiting for transfers between devices: 14.9 us -> 33.8 us  [shards(): table = lax.all_gather(owned.astype(BF), ('space', 'tm', 'spin'), axis=0)]
    dynamic_slice x11 -> x1, local copies, waits for them, and re-layouts: 14.5 us -> 0.79 us  [halo(): mine = lax.dynamic_slice_in_dim(plane, core, 1, 1)]
  transfers between devices with their start and end apart: 5 -> 5, of which waited for: 4 -> 3; matrix products, arithmetic and copies ran while one was open for 3% -> 10% of each run, Pallas kernels for 0% -> 24%
where the time goes in v1:
time: 141 us; the launch traced here: 140 us
  waiting for transfers between devices  57.6 us (41%)
  Pallas kernels  41.6 us (30%)
  local copies, waits for them, and re-layouts  15.8 us (11%)
  between operations  14.2 us (10%)
  other arithmetic  5.74 us (4%)
  starting transfers between devices  5.52 us (4%)
    all_gather x1, waiting for transfers between devices, shards(): table = lax.all_gather(owned.astype(BF), ('space', 'tm', 'spin'), axis=0)  33.8 us
    pallas_call x1, Pallas kernels, shards(): pl.pallas_call(functools.partial(local_kernel, plane_count, columns, scal...  33.1 us
    reduce_scatter x1, waiting for transfers between devices, shards(): owned = lax.psum_scatter(summed, 'space', scatter_dimension=2, tiled=True)  22.9 us
    reshape x2, local copies, waits for them, and re-layouts, shards(): strips = jnp.swapaxes(strips, 2, 3).reshape(slices, 1, 18, local_sites)  5.77 us
    ppermute x3, starting transfers between devices, shift_over(): lax.ppermute(array, axis, [(i, (i + by) % count) for i in range(count)])  5.44 us
    pallas_call x1, Pallas kernels, shards(): pl.pallas_call(functools.partial(contract_kernel, columns, 4), out_shape=...  5.4 us
    unnamed x15, local copies, waits for them, and re-layouts  3.24 us
    pallas_call x1, Pallas kernels, shards(): pl.pallas_call(functools.partial(boundary_kernel, columns, scaling), out_...  3.09 us
  transfers between devices with their start and end apart: 5, of which 3 were waited for; matrix products, arithmetic and copies ran while one was open for 10% of the time, Pallas kernels for 24%

profile of v1, /device:TPU:0, one launch (start us, length us, event | category | flops | bytes accessed | tf_op | source)
XLA Modules:
  0.0 140.4 jit_solution(8903601995334818696)
XLA Ops:
  7.2 0.0 copy-start.2
  7.2 0.0 reduce-scatter.2.cloned.1.call-start
  7.2 1.2 slice.9
  8.5 0.8 constant_dynamic-slice_fusion
  9.3 5.1 %collective-permute-start = (bf16[2,1,3,256,128]{4,3,2,1,0:T(8,128)(2,1)}, bf16[2,1,3,256,128]{4,3,2,1,0:T(8,128)(2,1)}, u32[]{:S(2)}, u32[]{:S(2)}) collective-permute-start(bf16[2,1,3,256,128]{4,3,2,1,0:T(8,128)(2,1)} %constant_dynamic-slice_fusion), channel_id=1, source_target_pairs={{0,12},{4,0},{8,4},{12,8},{1,13},{5,1},{9,5},{13,9},{2,14},{6,2},{... | collective-permute-start | bytes 1179656 | tf_op jit(solution)/shard_map/ppermute | solution.py:340
  14.4 0.0 copy-done.2
  14.4 0.5 copy.32
  14.9 0.7 slice.13
  15.7 1.9 %reshape_squeeze.3 = f32[2,18,8,16,16]{4,3,2,0,1:T(8,128)S(1)} reshape(f32[2,1,18,2048]{3,0,2,1:T(2,128)} %slice.13) | data formatting | bytes 589824 | tf_op jit(solution)/shard_map/reshape;squeeze | solution.py:371
  17.6 2.4 %copy.46 = f32[2,18,16,8,16]{4,3,2,1,0:T(8,128)} copy(f32[2,18,16,8,16]{4,2,3,0,1:T(8,128)S(1)} %bitcast.9) | data formatting | bytes 589824 | tf_op jit(solution)/shard_map/reshape | solution.py:372
  20.0 3.4 %reshape.48 = f32[2,1,18,2048]{3,2,1,0:T(8,128)S(1)} reshape(f32[2,18,16,8,16]{4,3,2,1,0:T(8,128)} %copy.46) | data formatting | bytes 589824 | tf_op jit(solution)/shard_map/reshape | solution.py:372
  23.3 0.0 copy-start.1
  23.3 0.3 copy.48
  23.7 0.1 pad_maximum_fusion.links_ref
  23.8 0.0 collective-permute-done
  23.8 0.1 collective-permute-start.1
  23.9 0.1 copy-done.1
  24.0 33.1 %local_gram.1.part_ref = f32[2,2,128,256]{3,2,1,0:T(8,128)S(1)} custom-call(s32[2]{0:T(128)S(1)} %copy-done.1, f32[2,8]{1,0:T(2,128)S(1)} %pad_maximum_fusion.2.phases, bf16[2,2,3,2048,128]{4,3,2,1,0:T(8,128)(2,1)} %v_ref.3, f32[2,3,18,2048]{3,2,1,0:T(8,128)S(1)} %pad_maximum_fusion.links_ref), custom_call_target="tpu_custom_call" | custom-call | flops 12999999488 | bytes 6291456 | tf_op jit(solution)/shard_map/local_gram/pallas_call | solution.py:375
  57.1 0.0 copy-start
  57.1 0.8 copy-done
  57.9 1.1 copy.36.links_ref
  59.0 0.0 collective-permute-done.1
  59.0 1.1 broadcast_select_fusion.1
  60.1 0.9 pad_maximum_fusion.1.above_ref
  61.1 0.0 copy-start.3
  61.1 0.0 copy-start.4
  61.1 3.1 %boundary.1 = f32[2,2,128,256]{3,2,1,0:T(8,128)} custom-call(s32[2]{0:T(128)} %dirs.3, bf16[2,2,3,2048,128]{4,3,2,1,0:T(8,128)(2,1)} %v_ref.3, bf16[2,3,2,3,3,2048]{5,4,3,2,1,0:T(4,128)(2,1)} %copy.36.links_ref, bf16[2,2,3,256,128]{4,3,2,1,0:T(8,128)(2,1)} %pad_maximum_fusion.1.above_ref, f32[2,2,128,256]{3,2,1,0:T(8,128)} %copy-done), custom_call_target="tpu_custom_call" | custom-call | tf_op jit(solution)/shard_map/boundary/pallas_call | solution.py:402
  64.2 0.0 reduce-scatter.2.cloned.1.call-update
  64.2 0.0 all-gather.3.cloned.1.call-start
  64.3 22.9 %reduce-scatter.2.cloned.1.call-done = f32[2,2,32,256]{3,2,1,0:T(8,128)} async-done(((f32[2,2,128,256]{3,2,1,0:T(8,128)}), f32[2,2,32,256]{3,2,1,0:T(8,128)}) %reduce-scatter.2.cloned.1.call-update) | async-done | bytes 131088 | tf_op jit(solution)/shard_map/reduce_scatter | solution.py:420
  87.1 1.5 %convert_element_type.19 = bf16[2,2,32,256]{3,2,1,0:T(8,128)(2,1)} convert(f32[2,2,32,256]{3,2,1,0:T(8,128)} %reduce-scatter.2.cloned.1.call-done) | non-fusion elementwise | flops 32768 | bytes 196608 | tf_op jit(solution)/shard_map/convert_element_type | solution.py:422
  88.7 0.0 all-gather.3.cloned.1.call-update
  88.7 0.0 copy-done.3
  88.7 0.1 copy.37
  88.8 0.0 copy-done.4
  88.8 0.1 copy.41
  88.9 0.5 compare_select_fusion.signs
  89.4 0.6 fusion.5.positions
  90.0 1.6 %reshape.42 = f32[2,2,32,2,128]{4,3,2,1,0:T(2,128)} reshape(f32[2,2,32,256]{3,2,1,0:T(8,128)} %reduce-scatter.2.cloned.1.call-done) | data formatting | bytes 262144 | tf_op jit(solution)/shard_map/reshape | solution.py:421
  91.7 33.8 %all-gather.3.cloned.1.call-done = bf16[32,2,32,256]{3,2,1,0:T(8,128)(2,1)} async-done(((bf16[2,2,32,256]{3,2,1,0:T(8,128)(2,1)}), bf16[32,2,32,256]{3,2,1,0:T(8,128)(2,1)}) %all-gather.3.cloned.1.call-update) | async-done | bytes 1048592 | tf_op jit(solution)/shard_map/all_gather | solution.py:422
  125.4 5.4 %contract.1 = f32[4,2,8,128]{3,2,1,0:T(8,128)} custom-call(s32[4,2]{1,0:T(4,128)} %fusion.5.positions, f32[8]{0:T(128)} %compare_select_fusion.signs, bf16[4,16,32,256]{3,2,1,0:T(8,128)(2,1)} %bitcast.10, bf16[4,16,32,256]{3,2,1,0:T(8,128)(2,1)} %bitcast.11, bf16[4,8,2,128,128]{4,3,2,1,0:T(8,128)(2,1)} %tau_ref.1), custom_call_target="tpu_custom_call" | custom-call | tf_op jit(solution)/shard_map/contract/pallas_call | solution.py:432
  130.8 0.9 reduce_sum.9
  131.7 0.3 collective-permute-start.2
  132.0 0.9 collective-permute-done.2
  132.9 0.7 copy.45
  (5 shorter events, 0.1 us)
Async XLA Ops:
  7.2 7.2 %copy-start.2 = (bf16[2,3,2,3,3,2048]{5,2,4,3,1,0:T(2,128)(2,1)S(1)}, bf16[2,3,2,3,3,2048]{5,2,4,3,1,0:T(2,128)(2,1)}, u32[]{:S(2)}) copy-start(bf16[2,3,2,3,3,2048]{5,2,4,3,1,0:T(2,128)(2,1)} %param.7) | copy-start | bytes 1327108
  7.2 80.0 %reduce-scatter.2.cloned.1.call-start = ((), (), s32[]{:S(2)}) async-start(), calls=%async_computation.1 | async-start | bytes 655360 | tf_op jit(solution)/shard_map/reduce_scatter | solution.py:420
  9.3 14.6 %collective-permute-start = (bf16[2,1,3,256,128]{4,3,2,1,0:T(8,128)(2,1)}, bf16[2,1,3,256,128]{4,3,2,1,0:T(8,128)(2,1)}, u32[]{:S(2)}, u32[]{:S(2)}) collective-permute-start(bf16[2,1,3,256,128]{4,3,2,1,0:T(8,128)(2,1)} %constant_dynamic-slice_fusion), channel_id=1, source_target_pairs={{0,12},{4,0},{8,4},{12,8},{1,13},{5,1},{9,5},{13,9},{2,14},{6,2},{... | collective-permute-start | bytes 1179656 | tf_op jit(solution)/shard_map/ppermute | solution.py:340
  23.3 0.7 copy-start.1
  23.8 35.2 %collective-permute-start.1 = (bf16[2,1,3,256,128]{4,3,2,1,0:T(8,128)(2,1)}, bf16[2,1,3,256,128]{4,3,2,1,0:T(8,128)(2,1)S(1)}, u32[]{:S(2)}, u32[]{:S(2)}) collective-permute-start(bf16[2,1,3,256,128]{4,3,2,1,0:T(8,128)(2,1)} %collective-permute-done), channel_id=1, source_target_pairs={{0,1},{1,0},{2,3},{3,2},{4,5},{5,4},{6,7},{7,6},{8,9},{9,8},{10,11... | collective-permute-start | bytes 1179656 | tf_op jit(solution)/shard_map/ppermute | solution.py:340
  57.1 0.8 copy-start
  61.1 27.6 %copy-start.3 = (s32[4,2]{0,1:T(2,128)S(1)}, s32[4,2]{0,1:T(2,128)}, u32[]{:S(2)}) copy-start(s32[4,2]{0,1:T(2,128)} %param.9) | copy-start | bytes 100
  61.1 27.7 %copy-start.4 = (s32[4,2]{0,1:T(2,128)S(1)}, s32[4,2]{0,1:T(2,128)}, u32[]{:S(2)}) copy-start(s32[4,2]{0,1:T(2,128)} %param.10) | copy-start | bytes 100
  64.2 61.2 %all-gather.3.cloned.1.call-start = ((), (), s32[]{:S(2)}) async-start(), calls=%async_computation.2 | async-start | bytes 1114112 | tf_op jit(solution)/shard_map/all_gather | solution.py:422
  131.7 1.2 collective-permute-start.2
Sparse Core Ops, SparseCore 0:
  64.3 22.7 reduce-scatter.1
  89.3 36.0 all-gather.2

commit v2 on v1

--- a/solution.py
+++ b/solution.py
@@ -13,6 +13,7 @@
 PLANE = PX * PY
 BF = jnp.bfloat16
 F32 = jnp.float32
+MESH = pl.DeviceIdType.MESH
 
 
 def neighbour_mask(group, shift_x):
@@ -247,10 +248,11 @@
 def boundary_kernel(columns, scaling, dirs, v_ref, links_ref, above_ref, part_ref, out_ref):
     op_slots = part_ref.shape[1]
     group = PLANE // 2
+    split = (out_ref.shape[0],) + out_ref.shape[3:]
     for slot in range(op_slots):
         @pl.when(dirs[slot] != 2)
         def _(slot=slot):
-            out_ref[0, slot] = part_ref[0, slot].astype(out_ref.dtype)
+            out_ref[:, 0, slot] = part_ref[0, slot].reshape(split).astype(out_ref.dtype)
 
         @pl.when(dirs[slot] == 2)
         def _(slot=slot):
@@ -276,9 +278,8 @@
                     axis=0,
                 )
                 total += gram(moved, other)
-            out_ref[0, slot] = (
-                part_ref[0, slot] + antihermitian(total, columns, scaling)
-            ).astype(out_ref.dtype)
+            whole = part_ref[0, slot] + antihermitian(total, columns, scaling)
+            out_ref[:, 0, slot] = whole.reshape(split).astype(out_ref.dtype)
 
 
 def contract_kernel(columns, quarter, positions, signs, source_ref, sink_ref, tau_ref, out_ref):
@@ -335,6 +336,136 @@
     out_ref[0, 1] = total_imag
 
 
+def reduce_kernel(layers, in_ref, sum_ref, half_ref, held, send_sem, recv_sem):
+    me = lax.axis_index("space")
+    barrier = pltpu.get_barrier_semaphore()
+    for d in range(1, layers):
+        pl.semaphore_signal(
+            barrier, inc=1, device_id={"space": lax.rem(me + d, layers)}, device_id_type=MESH
+        )
+    pl.semaphore_wait(barrier, layers - 1)
+    copies = []
+    for d in range(1, layers):
+        peer = lax.rem(me + d, layers)
+        copy = pltpu.make_async_remote_copy(
+            src_ref=in_ref.at[peer],
+            dst_ref=held.at[d - 1],
+            send_sem=send_sem.at[d - 1],
+            recv_sem=recv_sem.at[d - 1],
+            device_id={"space": peer},
+            device_id_type=MESH,
+        )
+        copy.start()
+        copies.append(copy)
+    total = in_ref[me]
+    for d in range(1, layers):
+        copies[d - 1].wait_recv()
+        total += held[d - 1]
+    sum_ref[...] = total
+    half_ref[...] = total.astype(BF)
+    for copy in copies:
+        copy.wait_send()
+
+
+def reduce_rows(blocks, layers):
+    shape = blocks.shape[1:]
+    return pl.pallas_call(
+        functools.partial(reduce_kernel, layers),
+        out_shape=(jax.ShapeDtypeStruct(shape, F32), jax.ShapeDtypeStruct(shape, BF)),
+        in_specs=[pl.BlockSpec(memory_space=pltpu.VMEM)],
+        out_specs=(pl.BlockSpec(memory_space=pltpu.VMEM),) * 2,
+        scratch_shapes=[
+            pltpu.VMEM((layers - 1,) + shape, F32),
+            pltpu.SemaphoreType.DMA((layers - 1,)),
+            pltpu.SemaphoreType.DMA((layers - 1,)),
+        ],
+        compiler_params=pltpu.CompilerParams(collective_id=0, has_side_effects=True),
+        name="reduce_rows",
+    )(blocks)
+
+
+def gather_kernel(
+    layers, times, cores, in_ref, out_ref, z_send, z_recv, t_send, t_recv, c_send, c_recv
+):
+    sizes = {"space": layers, "tm": times, "spin": cores}
+    here = {axis: lax.axis_index(axis) for axis in sizes}
+    barrier = pltpu.get_barrier_semaphore()
+    for axis, size in sizes.items():
+        for d in range(1, size):
+            pl.semaphore_signal(
+                barrier,
+                inc=1,
+                device_id={axis: lax.rem(here[axis] + d, size)},
+                device_id_type=MESH,
+            )
+    pl.semaphore_wait(barrier, layers + times + cores - 3)
+
+    def slot(d, e):
+        z = lax.rem(here["space"] + layers - d, layers)
+        t = lax.rem(here["tm"] + times - e, times)
+        return out_ref.at[z, t, here["spin"]]
+
+    def send(axis, distance, d, e, send_sem, recv_sem):
+        size = sizes[axis]
+        copy = pltpu.make_async_remote_copy(
+            src_ref=in_ref if d == 0 and e == 0 else slot(d, e),
+            dst_ref=slot(d, e),
+            send_sem=send_sem,
+            recv_sem=recv_sem,
+            device_id={axis: lax.rem(here[axis] + distance, size)},
+            device_id_type=MESH,
+        )
+        copy.start()
+        return copy
+
+    z_copies = [
+        send("space", d, 0, 0, z_send.at[d], z_recv.at[d]) for d in range(1, layers)
+    ]
+    t_copies, c_copies = {}, []
+
+    def pass_cores(d, e):
+        for f in range(1, cores):
+            c_copies.append(send("spin", f, d, e, c_send.at[d, e, f], c_recv.at[d, e, f]))
+
+    def pass_times(d):
+        for e in range(1, times):
+            t_copies[d, e] = send("tm", e, d, 0, t_send.at[d, e], t_recv.at[d, e])
+        pass_cores(d, 0)
+
+    pass_times(0)
+    out_ref[here["space"], here["tm"], here["spin"]] = in_ref[...]
+    for d in range(1, layers):
+        z_copies[d - 1].wait_recv()
+        pass_times(d)
+    for (d, e), copy in t_copies.items():
+        copy.wait_recv()
+        pass_cores(d, e)
+    for copy in c_copies:
+        copy.wait()
+    for copy in z_copies + list(t_copies.values()):
+        copy.wait_send()
+
+
+def gather_all(block, layers, times, cores):
+    dma = pltpu.SemaphoreType.DMA
+    return pl.pallas_call(
+        functools.partial(gather_kernel, layers, times, cores),
+        out_shape=jax.ShapeDtypeStruct((layers, times, cores) + block.shape, BF),
+        in_specs=[pl.BlockSpec(memory_space=pltpu.VMEM)],
+        out_specs=pl.BlockSpec(memory_space=pltpu.VMEM),
+        scratch_shapes=[
+            dma((layers,)),
+            dma((layers,)),
+            dma((layers, times)),
+            dma((layers, times)),
+            dma((layers, times, cores)),
+            dma((layers, times, cores)),
+        ],
+        compiler_params=pltpu.CompilerParams(collective_id=1, has_side_effects=True),
+        name="gather_all",
+    )(block)
+
+
 def shift_over(array, axis, by):
     count = lax.axis_size(axis)
     return lax.ppermute(array, axis, [(i, (i + by) % count) for i in range(count)])
@@ -399,9 +530,10 @@
     )(directions, phases, eigvecs, flat)
 
     last = plane_count - 1
+    rows = columns // layers
     summed = pl.pallas_call(
         functools.partial(boundary_kernel, columns, scaling),
-        out_shape=jax.ShapeDtypeStruct(partial.shape, F32),
+        out_shape=jax.ShapeDtypeStruct((layers, slices, op_slots, rows, 2 * columns), F32),
         grid_spec=pltpu.PrefetchScalarGridSpec(
             num_scalar_prefetch=1,
             grid=(slices,),
@@ -411,15 +543,16 @@
                 pl.BlockSpec((1, 2, 3, PLANE, columns), lambda t, d: (t, 0, 0, 0, 0)),
                 pl.BlockSpec((1, op_slots, columns, 2 * columns), lambda t, d: (t, 0, 0, 0)),
             ],
-            out_specs=pl.BlockSpec((1, op_slots, columns, 2 * columns), lambda t, d: (t, 0, 0, 0)),
+            out_specs=pl.BlockSpec(
+                (layers, 1, op_slots, rows, 2 * columns), lambda t, d: (0, t, 0, 0, 0)
+            ),
         ),
         name="boundary",
     )(directions, eigvecs, links, above, partial)
 
-    rows = columns // layers
-    owned = lax.psum_scatter(summed, "space", scatter_dimension=2, tiled=True)
-    elementals = owned.reshape(slices, op_slots, rows, 2, columns)
-    table = lax.all_gather(owned.astype(BF), ("space", "tm", "spin"), axis=0)
+    elementals, halves = reduce_rows(summed, layers)
+    elementals = elementals.reshape(slices, op_slots, rows, 2, columns)
+    table = gather_all(halves, layers, tm_size, spin_size)
     table = table.reshape(layers, tm_size * spin_size * slices * op_slots, rows, 2 * columns)
 
     position = (

time: 141 us -> 96.3 us (0.68)
  waiting for transfers between devices: 57.6 us -> 0.1 us
  Pallas kernels: 41.6 us -> 69.2 us
  between operations: 14.2 us -> 0.79 us
  other arithmetic: 5.74 us -> 4.14 us
    all_gather x1 -> x0, waiting for transfers between devices: 33.8 us -> none  [shards(): table = lax.all_gather(owned.astype(BF), ('space', 'tm', 'spin'), axis=0)]
    pallas_call x0 -> x2, Pallas kernels: none -> 27.7 us  [the longest x1 16.3 us: gather_all(): pl.pallas_call(functools.partial(gather_kernel, layers, times, cores), ou...]
    reduce_scatter x1 -> x0, waiting for transfers between devices: 22.9 us -> none  [shards(): owned = lax.psum_scatter(summed, 'space', scatter_dimension=2, tiled=True)]
    convert_element_type x1 -> x0, other arithmetic: 1.54 us -> none  [shards(): table = lax.all_gather(owned.astype(BF), ('space', 'tm', 'spin'), axis=0)]
    unnamed x15 -> x17, local copies, waits for them, and re-layouts: 3.24 us -> 3.22 us
  transfers between devices with their start and end apart: 5 -> 3, of which waited for: 3 -> 1; matrix products, arithmetic and copies ran while one was open for 10% -> 13% of each run, Pallas kernels for 24% -> 35%
where the time goes in v2:
time: 96.3 us; the launch traced here: 94.7 us
  Pallas kernels  69.2 us (72%)
  local copies, waits for them, and re-layouts  14.9 us (15%)
  starting transfers between devices  5.56 us (6%)
  other arithmetic  4.14 us (4%)
    pallas_call x1, Pallas kernels, shards(): pl.pallas_call(functools.partial(local_kernel, plane_count, columns, scal...  33.1 us
    pallas_call x1, Pallas kernels, gather_all(): pl.pallas_call(functools.partial(gather_kernel, layers, times, cores), ou...  16.3 us
    pallas_call x1, Pallas kernels, reduce_rows(): pl.pallas_call(functools.partial(reduce_kernel, layers), out_shape=(jax.S...  11.4 us
    reshape x2, local copies, waits for them, and re-layouts, shards(): strips = jnp.swapaxes(strips, 2, 3).reshape(slices, 1, 18, local_sites)  5.78 us
    ppermute x3, starting transfers between devices, shift_over(): lax.ppermute(array, axis, [(i, (i + by) % count) for i in range(count)])  5.56 us
    pallas_call x1, Pallas kernels, shards(): pl.pallas_call(functools.partial(contract_kernel, columns, 4), out_shape=...  5.53 us
    unnamed x17, local copies, waits for them, and re-layouts  3.22 us
    pallas_call x1, Pallas kernels, shards(): pl.pallas_call(functools.partial(boundary_kernel, columns, scaling), out_...  2.95 us
  transfers between devices with their start and end apart: 3, of which 1 were waited for; matrix products, arithmetic and copies ran while one was open for 13% of the time, Pallas kernels for 35%

profile of v2, /device:TPU:0, one launch (start us, length us, event | category | flops | bytes accessed | tf_op | source)
XLA Modules:
  0.0 94.7 jit_solution(13600691912460472717)
XLA Ops:
  0.6 0.0 copy-start.2
  0.6 1.2 %slice.9 = bf16[2,2,3,256,128]{4,3,2,1,0:T(8,128)(2,1)S(1)} slice(bf16[2,2,3,2048,128]{4,3,2,1,0:T(8,128)(2,1)} %v_ref.3), slice={[0:2], [0:2], [0:3], [0:256], [0:128]} | slice | bytes 1572864 | tf_op jit(solution)/shard_map/slice | solution.py:475
  1.9 0.8 constant_dynamic-slice_fusion
  2.7 5.1 %collective-permute-start = (bf16[2,1,3,256,128]{4,3,2,1,0:T(8,128)(2,1)}, bf16[2,1,3,256,128]{4,3,2,1,0:T(8,128)(2,1)}, u32[]{:S(2)}, u32[]{:S(2)}) collective-permute-start(bf16[2,1,3,256,128]{4,3,2,1,0:T(8,128)(2,1)} %constant_dynamic-slice_fusion), channel_id=1, source_target_pairs={{0,12},{4,0},{8,4},{12,8},{1,13},{5,1},{9,5},{13,9},{2,14},{6,2},{... | collective-permute-start | bytes 1179656 | tf_op jit(solution)/shard_map/ppermute | solution.py:471
  7.8 0.0 copy-done.2
  7.8 0.5 copy.32
  8.3 0.7 slice.13
  9.1 1.9 %reshape_squeeze.3 = f32[2,18,8,16,16]{4,3,2,0,1:T(8,128)S(1)} reshape(f32[2,1,18,2048]{3,0,2,1:T(2,128)} %slice.13) | data formatting | bytes 589824 | tf_op jit(solution)/shard_map/reshape;squeeze | solution.py:502
  11.0 2.4 %copy.46 = f32[2,18,16,8,16]{4,3,2,1,0:T(8,128)} copy(f32[2,18,16,8,16]{4,2,3,0,1:T(8,128)S(1)} %bitcast.9) | data formatting | bytes 589824 | tf_op jit(solution)/shard_map/reshape | solution.py:503
  13.4 3.4 %reshape.46 = f32[2,1,18,2048]{3,2,1,0:T(8,128)S(1)} reshape(f32[2,18,16,8,16]{4,3,2,1,0:T(8,128)} %copy.46) | data formatting | bytes 589824 | tf_op jit(solution)/shard_map/reshape | solution.py:503
  16.8 0.0 copy-start.1
  16.8 0.3 copy.48
  17.2 0.1 pad_maximum_fusion.links_ref
  17.3 0.0 copy-start.4
  17.3 0.0 copy-start.5
  17.3 0.0 collective-permute-done
  17.3 0.1 collective-permute-start.1
  17.4 0.1 copy-done.1
  17.4 33.1 %local_gram.1.part_ref = f32[2,2,128,256]{3,2,1,0:T(8,128)S(1)} custom-call(s32[2]{0:T(128)S(1)} %copy-done.1, f32[2,8]{1,0:T(2,128)S(1)} %pad_maximum_fusion.2.phases, bf16[2,2,3,2048,128]{4,3,2,1,0:T(8,128)(2,1)} %v_ref.3, f32[2,3,18,2048]{3,2,1,0:T(8,128)S(1)} %pad_maximum_fusion.links_ref), custom_call_target="tpu_custom_call" | custom-call | flops 12999999488 | bytes 6291456 | tf_op jit(solution)/shard_map/local_gram/pallas_call | solution.py:506
  50.5 0.0 copy-start
  50.5 0.8 copy-done
  51.3 1.1 %copy.36.links_ref = bf16[2,3,2,3,3,2048]{5,4,3,2,1,0:T(4,128)(2,1)} copy(bf16[2,3,2,3,3,2048]{5,2,4,3,1,0:T(2,128)(2,1)S(1)} %copy-done.2) | data formatting | bytes 884736 | tf_op args[1]
  52.5 0.0 copy-done.4
  52.5 0.1 copy.37
  52.6 0.0 copy-done.5
  52.6 0.1 copy.41
  52.7 0.5 compare_select_fusion.signs
  53.2 0.6 fusion.5.positions
  53.8 0.0 collective-permute-done.1
  53.8 1.1 %broadcast_select_fusion.1 = (bf16[2,1,3,256,128]{4,3,2,1,0:T(8,128)(2,1)S(1)}, bf16[2,1,3,256,128]{4,3,2,1,0:T(8,128)(2,1)S(1)}) fusion(bf16[2,1,3,256,128]{4,3,2,1,0:T(8,128)(2,1)} %collective-permute-done, bf16[2,1,3,256,128]{4,3,2,1,0:T(8,128)(2,1)S(1)} %collective-permute-done.1, pred[]{:T(512)S(6)} %eq.12), kind=kLoop, calls=%fused_computation.3 | loop fusion | flops 393216 | bytes 1572865 | tf_op jit(solution)/shard_map/jit(_where)/select_n | solution.py:483
  54.8 1.0 %pad_maximum_fusion.1.above_ref = bf16[2,2,3,256,128]{4,3,2,1,0:T(8,128)(2,1)} fusion(bf16[2,1,3,256,128]{4,3,2,1,0:T(8,128)(2,1)S(1)} %get-tuple-element.9, bf16[2,1,3,256,128]{4,3,2,1,0:T(8,128)(2,1)S(1)} %get-tuple-element.8), kind=kLoop, calls=%fused_computation.1 | loop fusion | flops 393216 | bytes 1572864 | tf_op jit(solution)/shard_map/concatenate | solution.py:482
  55.8 2.9 %boundary.1.in_ref = f32[4,2,2,32,256]{4,3,2,1,0:T(8,128)} custom-call(s32[2]{0:T(128)} %dirs.3, bf16[2,2,3,2048,128]{4,3,2,1,0:T(8,128)(2,1)} %v_ref.3, bf16[2,3,2,3,3,2048]{5,4,3,2,1,0:T(4,128)(2,1)} %copy.36.links_ref, bf16[2,2,3,256,128]{4,3,2,1,0:T(8,128)(2,1)} %pad_maximum_fusion.1.above_ref, f32[2,2,128,256]{3,2,1,0:T(8,128)} %copy-done), custom_call_target="tpu_custom_call" | custom-call | tf_op jit(solution)/shard_map/boundary/pallas_call | solution.py:534
  58.7 11.4 %reduce_rows.1 = (f32[2,2,32,256]{3,2,1,0:T(8,128)}, bf16[2,2,32,256]{3,2,1,0:T(8,128)(2,1)}) custom-call(f32[4,2,2,32,256]{4,3,2,1,0:T(8,128)} %boundary.1.in_ref), custom_call_target="tpu_custom_call" | custom-call | tf_op jit(solution)/shard_map/reduce_rows/pallas_call | solution.py:372
  70.1 16.3 %gather_all.1 = bf16[4,2,2,2,2,32,256]{6,5,4,3,2,1,0:T(8,128)(2,1)} custom-call(bf16[2,2,32,256]{3,2,1,0:T(8,128)(2,1)} %get-tuple-element.5.in_ref), custom_call_target="tpu_custom_call" | custom-call | tf_op jit(solution)/shard_map/gather_all/pallas_call | solution.py:451
  86.4 0.0 copy-start.3
  86.4 5.5 %contract.1 = f32[4,2,8,128]{3,2,1,0:T(8,128)} custom-call(s32[4,2]{1,0:T(4,128)} %fusion.5.positions, f32[8]{0:T(128)} %compare_select_fusion.signs, bf16[4,16,32,256]{3,2,1,0:T(8,128)(2,1)} %bitcast.10, bf16[4,16,32,256]{3,2,1,0:T(8,128)(2,1)} %bitcast.11, bf16[4,8,2,128,128]{4,3,2,1,0:T(8,128)(2,1)} %tau_ref.1), custom_call_target="tpu_custom_call" | custom-call | tf_op jit(solution)/shard_map/contract/pallas_call | solution.py:565
  92.0 0.9 reduce_sum.9
  92.8 0.4 collective-permute-start.2
  93.3 0.0 copy-done.3
  93.3 0.7 reshape.42
  94.0 0.1 collective-permute-done.2
  94.1 0.7 copy.45
  (5 shorter events, 0.1 us)
Async XLA Ops:
  0.6 7.2 %copy-start.2 = (bf16[2,3,2,3,3,2048]{5,2,4,3,1,0:T(2,128)(2,1)S(1)}, bf16[2,3,2,3,3,2048]{5,2,4,3,1,0:T(2,128)(2,1)}, u32[]{:S(2)}) copy-start(bf16[2,3,2,3,3,2048]{5,2,4,3,1,0:T(2,128)(2,1)} %param.7) | copy-start | bytes 1327108
  2.7 14.6 %collective-permute-start = (bf16[2,1,3,256,128]{4,3,2,1,0:T(8,128)(2,1)}, bf16[2,1,3,256,128]{4,3,2,1,0:T(8,128)(2,1)}, u32[]{:S(2)}, u32[]{:S(2)}) collective-permute-start(bf16[2,1,3,256,128]{4,3,2,1,0:T(8,128)(2,1)} %constant_dynamic-slice_fusion), channel_id=1, source_target_pairs={{0,12},{4,0},{8,4},{12,8},{1,13},{5,1},{9,5},{13,9},{2,14},{6,2},{... | collective-permute-start | bytes 1179656 | tf_op jit(solution)/shard_map/ppermute | solution.py:471
  16.8 0.7 copy-start.1
  17.3 35.2 %copy-start.4 = (s32[4,2]{0,1:T(2,128)S(1)}, s32[4,2]{0,1:T(2,128)}, u32[]{:S(2)}) copy-start(s32[4,2]{0,1:T(2,128)} %param.9) | copy-start | bytes 100
  17.3 35.3 %copy-start.5 = (s32[4,2]{0,1:T(2,128)S(1)}, s32[4,2]{0,1:T(2,128)}, u32[]{:S(2)}) copy-start(s32[4,2]{0,1:T(2,128)} %param.10) | copy-start | bytes 100
  17.3 36.5 %collective-permute-start.1 = (bf16[2,1,3,256,128]{4,3,2,1,0:T(8,128)(2,1)}, bf16[2,1,3,256,128]{4,3,2,1,0:T(8,128)(2,1)S(1)}, u32[]{:S(2)}, u32[]{:S(2)}) collective-permute-start(bf16[2,1,3,256,128]{4,3,2,1,0:T(8,128)(2,1)} %collective-permute-done), channel_id=1, source_target_pairs={{0,1},{1,0},{2,3},{3,2},{4,5},{5,4},{6,7},{7,6},{8,9},{9,8},{10,11... | collective-permute-start | bytes 1179656 | tf_op jit(solution)/shard_map/ppermute | solution.py:471
  50.5 0.8 copy-start
  86.4 6.8 %copy-start.3 = (f32[2,2,32,256]{3,2,1,0:T(8,128)S(1)}, f32[2,2,32,256]{3,2,1,0:T(8,128)}, u32[]{:S(2)}) copy-start(f32[2,2,32,256]{3,2,1,0:T(8,128)} %get-tuple-element.4) | copy-start | bytes 393220
  92.8 1.2 %collective-permute-start.2 = (f32[4,2]{1,0:T(4,128)S(1)}, f32[4,2]{1,0:T(4,128)S(1)}, u32[]{:S(2)}, u32[]{:S(2)}) collective-permute-start(f32[4,2]{1,0:T(4,128)S(1)} %broadcast_multiply_fusion), channel_id=1, source_target_pairs={{0,1},{1,0},{2,3},{3,2},{4,5},{5,4},{6,7},{7,6},{8,9},{9,8},{10,11... | collective-permute-start | bytes 104 | tf_op jit(solution)/shard_map/ppermute | solution.py:471

commit v3 on v2

--- a/solution.py
+++ b/solution.py
@@ -190,12 +190,19 @@
 
     @pl.when(code == 2)
     def _():
+        lane = lax.broadcasted_iota(jnp.int32, (18, group), 1)
         mask_up = ones_where(row == col - strip)
         mask_down = ones_where(row == col + strip)
 
         def step(n, carry):
-            start = pl.multiple_of(n * group, group)
-            field = links_ref[0, 0, :, pl.ds(start, group)]
+            per_chunk = group // strip
+            chunk = pl.multiple_of((n // per_chunk) * group, group)
+            turn = lax.rem(n, per_chunk)
+            field = jnp.zeros((18, group), F32)
+            for z in range(plane_count):
+                line = links_ref[0, 0, :, pl.ds(z * PLANE + chunk, group)]
+                shift = lax.rem(z + per_chunk - turn, per_chunk) * strip
+                field = jnp.where(lane // strip == z, pltpu.roll(line, shift, 1), field)
             ahead = pltpu.roll(field, strip, 1)
             matrix = stencil(ahead.astype(BF), field.astype(BF), mask_up, mask_down)
             places = [
@@ -473,15 +480,7 @@
 
 def halo(eigvecs):
     plane = eigvecs[:, :, :, :PLANE]
-    if lax.axis_size("spin") != 2:
-        return shift_over(plane, "space", -1)
-    core = lax.axis_index("spin")
-    mine = lax.dynamic_slice_in_dim(plane, core, 1, 1)
-    mine = shift_over(mine, "space", -1)
-    theirs = shift_over(mine, "spin", 1)
-    return jnp.concatenate(
-        [jnp.where(core == 0, mine, theirs), jnp.where(core == 0, theirs, mine)], axis=1
-    )
+    return shift_over(plane, "space", -1)
 
 
 def shards(eigvecs, links, directions, pair_list, pair_operators, perambulators):
@@ -499,9 +498,6 @@
     above = halo(eigvecs)
 
     flat = links.astype(F32).reshape(slices, 3, 18, local_sites)
-    strips = flat[:, 2].reshape(slices, 18, plane_count, -1, PLANE // 2 // plane_count)
-    strips = jnp.swapaxes(strips, 2, 3).reshape(slices, 1, 18, local_sites)
-    flat = jnp.concatenate([flat[:, :2], strips], axis=1)
 
     partial = pl.pallas_call(
         functools.partial(local_kernel, plane_count, columns, scaling),

time: 96.3 us -> 91 us (0.945)
  local copies, waits for them, and re-layouts: 14.9 us -> 8.59 us
  Pallas kernels: 69.2 us -> 72.7 us
  other arithmetic: 4.14 us -> 2.04 us
    reshape x2 -> x0, local copies, waits for them, and re-layouts: 5.78 us -> none  [shards(): strips = jnp.swapaxes(strips, 2, 3).reshape(slices, 1, 18, local_sites)]
    pallas_call x1, Pallas kernels: 33.1 us -> 36.4 us  [shards(): pl.pallas_call(functools.partial(local_kernel, plane_count, columns, scal...]
    another operation x1 -> x0, local copies, waits for them, and re-layouts: 1.9 us -> none  [shards(): flat[:, 2].reshape(slices, 18, plane_count, -1, PLANE // 2 // plane_count)]
    pallas_call x1, Pallas kernels: 2.95 us -> 4.81 us  [shards(): pl.pallas_call(functools.partial(boundary_kernel, columns, scaling), out_...]
    reshape x1 -> x2, local copies, waits for them, and re-layouts: 0.49 us -> 2.06 us  [shards(): flat = links.astype(F32).reshape(slices, 3, 18, local_sites)]
    select_n x1 -> x0, other arithmetic: 1.05 us -> none  [halo(): jnp.where(core == 0, mine, theirs)]
    concatenate x2 -> x0, other arithmetic: 1.05 us -> none  [the longest x1 0.95 us: halo(): jnp.concatenate([jnp.where(core == 0, mine, theirs), jnp.where(core == 0,...]
    unnamed x17 -> x18, local copies, waits for them, and re-layouts: 3.22 us -> 3.68 us
  transfers between devices with their start and end apart: 3 -> 2, of which waited for: 1 -> 1; matrix products, arithmetic and copies ran while one was open for 13% -> 6% of each run, Pallas kernels for 35% -> 41%
where the time goes in v3:
time: 91 us; the launch traced here: 89.7 us
  Pallas kernels  72.7 us (80%)
  local copies, waits for them, and re-layouts  8.59 us (9%)
  starting transfers between devices  5.49 us (6%)
  other arithmetic  2.04 us (2%)
    pallas_call x1, Pallas kernels, shards(): pl.pallas_call(functools.partial(local_kernel, plane_count, columns, scal...  36.4 us
    pallas_call x1, Pallas kernels, gather_all(): pl.pallas_call(functools.partial(gather_kernel, layers, times, cores), ou...  15.5 us
    pallas_call x1, Pallas kernels, reduce_rows(): pl.pallas_call(functools.partial(reduce_kernel, layers), out_shape=(jax.S...  10.5 us
    pallas_call x1, Pallas kernels, shards(): pl.pallas_call(functools.partial(contract_kernel, columns, 4), out_shape=...  5.54 us
    ppermute x2, starting transfers between devices, shift_over(): lax.ppermute(array, axis, [(i, (i + by) % count) for i in range(count)])  5.49 us
    pallas_call x1, Pallas kernels, shards(): pl.pallas_call(functools.partial(boundary_kernel, columns, scaling), out_...  4.81 us
    unnamed x18, local copies, waits for them, and re-layouts  3.68 us
    slice x1, local copies, waits for them, and re-layouts, halo(): plane = eigvecs[:, :, :, :PLANE]  2.13 us
  transfers between devices with their start and end apart: 2, of which 1 were waited for; matrix products, arithmetic and copies ran while one was open for 6% of the time, Pallas kernels for 41%

profile of v3, /device:TPU:0, one launch (start us, length us, event | category | flops | bytes accessed | tf_op | source)
XLA Modules:
  0.0 89.7 jit_solution(401899645551778487)
XLA Ops:
  0.6 0.0 copy-start.2
  0.6 2.1 %slice.3 = bf16[2,2,3,256,128]{4,3,2,1,0:T(8,128)(2,1)} slice(bf16[2,2,3,2048,128]{4,3,2,1,0:T(8,128)(2,1)} %v_ref.3), slice={[0:2], [0:2], [0:3], [0:256], [0:128]} | slice | bytes 1572864 | tf_op jit(solution)/shard_map/slice | solution.py:482
  2.8 5.1 %collective-permute-start = (bf16[2,2,3,256,128]{4,3,2,1,0:T(8,128)(2,1)}, bf16[2,2,3,256,128]{4,3,2,1,0:T(8,128)(2,1)S(1)}, u32[]{:S(2)}, u32[]{:S(2)}) collective-permute-start(bf16[2,2,3,256,128]{4,3,2,1,0:T(8,128)(2,1)} %slice.3), channel_id=1, source_target_pairs={{0,12},{4,0},{8,4},{12,8},{1,13},{5,1},{9,5},{13,9},{2,14},{6,2},{... | collective-permute-start | bytes 2359304 | tf_op jit(solution)/shard_map/ppermute | solution.py:478
  7.8 0.0 copy-start.5
  7.8 0.0 copy-start.6
  7.9 0.0 copy-start.1
  7.9 1.5 %copy.29 = f32[2,3,2,3,3,2048]{5,0,4,3,2,1:T(2,128)S(1)} copy(bf16[2,3,2,3,3,2048]{5,2,4,3,1,0:T(2,128)(2,1)} %param.7) | data formatting | bytes 1327104 | tf_op jit(solution)/shard_map/reshape | solution.py:500
  9.4 0.0 copy-done.2
  9.4 1.2 %copy.31.links_ref = bf16[2,3,2,3,3,2048]{5,4,3,2,1,0:T(4,128)(2,1)} copy(bf16[2,3,2,3,3,2048]{5,2,4,3,1,0:T(2,128)(2,1)S(1)} %copy-done.2) | data formatting | bytes 884736 | tf_op args[1]
  10.6 0.5 copy.30.links_ref
  11.1 0.5 compare_select_fusion.signs
  11.7 0.0 copy-done.5
  11.7 0.1 copy.32
  11.8 0.0 copy-done.6
  11.8 0.1 copy.36
  11.9 0.6 fusion.5.positions
  12.5 0.0 copy-done.1
  12.5 36.4 %local_gram.1.part_ref = f32[2,2,128,256]{3,2,1,0:T(8,128)S(1)} custom-call(s32[2]{0:T(128)S(1)} %copy-done.1, f32[2,8]{1,0:T(2,128)S(1)} %pad_maximum_fusion.phases, bf16[2,2,3,2048,128]{4,3,2,1,0:T(8,128)(2,1)} %v_ref.3, f32[2,3,18,2048]{3,2,1,0:T(8,128)S(1)} %copy.30.links_ref), custom_call_target="tpu_custom_call" | custom-call | flops 12999999488 | bytes 6291456 | tf_op jit(solution)/shard_map/local_gram/pallas_call | solution.py:502
  48.9 0.0 copy-start
  48.9 0.8 copy-done
  49.7 0.0 collective-permute-done.above_ref
  49.7 0.0 copy-start.3
  49.7 0.9 copy-done.3
  50.6 4.8 %boundary.1.in_ref = f32[4,2,2,32,256]{4,3,2,1,0:T(8,128)} custom-call(s32[2]{0:T(128)} %dirs.3, bf16[2,2,3,2048,128]{4,3,2,1,0:T(8,128)(2,1)} %v_ref.3, bf16[2,3,2,3,3,2048]{5,4,3,2,1,0:T(4,128)(2,1)} %copy.31.links_ref, bf16[2,2,3,256,128]{4,3,2,1,0:T(8,128)(2,1)} %copy-done.3, f32[2,2,128,256]{3,2,1,0:T(8,128)} %copy-done), custom_call_target="tpu_custom_call" | custom-call | tf_op jit(solution)/shard_map/boundary/pallas_call | solution.py:530
  55.4 10.5 %reduce_rows.1 = (f32[2,2,32,256]{3,2,1,0:T(8,128)}, bf16[2,2,32,256]{3,2,1,0:T(8,128)(2,1)}) custom-call(f32[4,2,2,32,256]{4,3,2,1,0:T(8,128)} %boundary.1.in_ref), custom_call_target="tpu_custom_call" | custom-call | tf_op jit(solution)/shard_map/reduce_rows/pallas_call | solution.py:379
  65.9 15.5 %gather_all.1 = bf16[4,2,2,2,2,32,256]{6,5,4,3,2,1,0:T(8,128)(2,1)} custom-call(bf16[2,2,32,256]{3,2,1,0:T(8,128)(2,1)} %get-tuple-element.5.in_ref), custom_call_target="tpu_custom_call" | custom-call | tf_op jit(solution)/shard_map/gather_all/pallas_call | solution.py:458
  81.4 0.0 copy-start.4
  81.4 5.5 %contract.1 = f32[4,2,8,128]{3,2,1,0:T(8,128)} custom-call(s32[4,2]{1,0:T(4,128)} %fusion.5.positions, f32[8]{0:T(128)} %compare_select_fusion.signs, bf16[4,16,32,256]{3,2,1,0:T(8,128)(2,1)} %bitcast.4, bf16[4,16,32,256]{3,2,1,0:T(8,128)(2,1)} %bitcast.5, bf16[4,8,2,128,128]{4,3,2,1,0:T(8,128)(2,1)} %tau_ref.1), custom_call_target="tpu_custom_call" | custom-call | tf_op jit(solution)/shard_map/contract/pallas_call | solution.py:561
  86.9 0.9 reduce_sum.9
  87.8 0.4 collective-permute-start.1
  88.2 0.0 copy-done.4
  88.2 0.7 reshape.37
  88.9 0.1 collective-permute-done.1
  89.0 0.7 copy.40
  (4 shorter events, 0.1 us)
Async XLA Ops:
  0.6 8.8 %copy-start.2 = (bf16[2,3,2,3,3,2048]{5,2,4,3,1,0:T(2,128)(2,1)S(1)}, bf16[2,3,2,3,3,2048]{5,2,4,3,1,0:T(2,128)(2,1)}, u32[]{:S(2)}) copy-start(bf16[2,3,2,3,3,2048]{5,2,4,3,1,0:T(2,128)(2,1)} %param.7) | copy-start | bytes 1327108
  2.8 46.9 %collective-permute-start = (bf16[2,2,3,256,128]{4,3,2,1,0:T(8,128)(2,1)}, bf16[2,2,3,256,128]{4,3,2,1,0:T(8,128)(2,1)S(1)}, u32[]{:S(2)}, u32[]{:S(2)}) collective-permute-start(bf16[2,2,3,256,128]{4,3,2,1,0:T(8,128)(2,1)} %slice.3), channel_id=1, source_target_pairs={{0,12},{4,0},{8,4},{12,8},{1,13},{5,1},{9,5},{13,9},{2,14},{6,2},{... | collective-permute-start | bytes 2359304 | tf_op jit(solution)/shard_map/ppermute | solution.py:478
  7.8 3.8 %copy-start.5 = (s32[4,2]{0,1:T(2,128)S(1)}, s32[4,2]{0,1:T(2,128)}, u32[]{:S(2)}) copy-start(s32[4,2]{0,1:T(2,128)} %param.9) | copy-start | bytes 100
  7.8 3.9 %copy-start.6 = (s32[4,2]{0,1:T(2,128)S(1)}, s32[4,2]{0,1:T(2,128)}, u32[]{:S(2)}) copy-start(s32[4,2]{0,1:T(2,128)} %param.10) | copy-start | bytes 100
  7.9 4.6 %copy-start.1 = (s32[2]{0:T(128)S(1)}, s32[2]{0:T(128)}, u32[]{:S(2)}) copy-start(s32[2]{0:T(128)} %dirs.3) | copy-start | bytes 28
  48.9 0.8 copy-start
  49.7 0.9 copy-start.3
  81.4 6.8 %copy-start.4 = (f32[2,2,32,256]{3,2,1,0:T(8,128)S(1)}, f32[2,2,32,256]{3,2,1,0:T(8,128)}, u32[]{:S(2)}) copy-start(f32[2,2,32,256]{3,2,1,0:T(8,128)} %get-tuple-element.4) | copy-start | bytes 393220
  87.8 1.2 %collective-permute-start.1 = (f32[4,2]{1,0:T(4,128)S(1)}, f32[4,2]{1,0:T(4,128)S(1)}, u32[]{:S(2)}, u32[]{:S(2)}) collective-permute-start(f32[4,2]{1,0:T(4,128)S(1)} %broadcast_multiply_fusion), channel_id=1, source_target_pairs={{0,1},{1,0},{2,3},{3,2},{4,5},{5,4},{6,7},{7,6},{8,9},{9,8},{10,11... | collective-permute-start | bytes 104 | tf_op jit(solution)/shard_map/ppermute | solution.py:478

commit v4 on v3

--- a/solution.py
+++ b/solution.py
@@ -194,15 +194,15 @@
         mask_up = ones_where(row == col - strip)
         mask_down = ones_where(row == col + strip)
 
-        def step(n, carry):
-            per_chunk = group // strip
-            chunk = pl.multiple_of((n // per_chunk) * group, group)
+        per_chunk = group // strip
+
+        def step(n, lines):
             turn = lax.rem(n, per_chunk)
-            field = jnp.zeros((18, group), F32)
-            for z in range(plane_count):
-                line = links_ref[0, 0, :, pl.ds(z * PLANE + chunk, group)]
-                shift = lax.rem(z + per_chunk - turn, per_chunk) * strip
-                field = jnp.where(lane // strip == z, pltpu.roll(line, shift, 1), field)
+            place_of = lax.rem(lane // strip + per_chunk - turn, per_chunk)
+            field = lines[0]
+            for z in range(1, plane_count):
+                field = jnp.where(place_of == z, lines[z], field)
+            field = pltpu.roll(field, lax.rem(per_chunk - turn, per_chunk) * strip, 1)
             ahead = pltpu.roll(field, strip, 1)
             matrix = stencil(ahead.astype(BF), field.astype(BF), mask_up, mask_down)
             places = [
@@ -218,9 +218,18 @@
                 for z, place in enumerate(places):
                     low = a * group + z * strip
                     moved[a, pl.ds(place, strip), :] = value[low : low + strip]
-            return carry
-
-        lax.fori_loop(0, groups, step, 0)
+            return lines
+
+        for chunk in range(groups // per_chunk):
+            lines = tuple(
+                pltpu.roll(
+                    links_ref[0, 0, :, pl.ds(z * PLANE + chunk * group, group)],
+                    z * strip % group,
+                    1,
+                )
+                for z in range(plane_count)
+            )
+            lax.fori_loop(chunk * per_chunk, (chunk + 1) * per_chunk, step, lines)
 
     @pl.when(code == 3)
     def _():

time: 91 us -> 90.3 us (level); the launches traced: 89.7 us -> 90.7 us
  Pallas kernels: 72.7 us -> 73.8 us
    pallas_call x1, Pallas kernels: 36.4 us -> 37.5 us  [shards(): pl.pallas_call(functools.partial(local_kernel, plane_count, columns, scal...]
where the time goes in v4:
time: 90.3 us; the launch traced here: 90.7 us
  Pallas kernels  73.8 us (82%)
  local copies, waits for them, and re-layouts  8.59 us (10%)
  starting transfers between devices  5.49 us (6%)
  other arithmetic  2.04 us (2%)
    pallas_call x1, Pallas kernels, shards(): pl.pallas_call(functools.partial(local_kernel, plane_count, columns, scal...  37.5 us
    pallas_call x1, Pallas kernels, gather_all(): pl.pallas_call(functools.partial(gather_kernel, layers, times, cores), ou...  15.5 us
    pallas_call x1, Pallas kernels, reduce_rows(): pl.pallas_call(functools.partial(reduce_kernel, layers), out_shape=(jax.S...  10.5 us
    pallas_call x1, Pallas kernels, shards(): pl.pallas_call(functools.partial(contract_kernel, columns, 4), out_shape=...  5.55 us
    ppermute x2, starting transfers between devices, shift_over(): lax.ppermute(array, axis, [(i, (i + by) % count) for i in range(count)])  5.49 us
    pallas_call x1, Pallas kernels, shards(): pl.pallas_call(functools.partial(boundary_kernel, columns, scaling), out_...  4.81 us
    unnamed x18, local copies, waits for them, and re-layouts  3.68 us
    slice x1, local copies, waits for them, and re-layouts, halo(): plane = eigvecs[:, :, :, :PLANE]  2.13 us
  transfers between devices with their start and end apart: 2, of which 1 were waited for; matrix products, arithmetic and copies ran while one was open for 6% of the time, Pallas kernels for 41%

profile of v4, /device:TPU:0, one launch (start us, length us, event | category | flops | bytes accessed | tf_op | source)
XLA Modules:
  0.0 90.7 jit_solution(10795972482243140707)
XLA Ops:
  0.6 0.0 copy-start.2
  0.6 2.1 %slice.3 = bf16[2,2,3,256,128]{4,3,2,1,0:T(8,128)(2,1)} slice(bf16[2,2,3,2048,128]{4,3,2,1,0:T(8,128)(2,1)} %v_ref.3), slice={[0:2], [0:2], [0:3], [0:256], [0:128]} | slice | bytes 1572864 | tf_op jit(solution)/shard_map/slice | solution.py:491
  2.8 5.1 %collective-permute-start = (bf16[2,2,3,256,128]{4,3,2,1,0:T(8,128)(2,1)}, bf16[2,2,3,256,128]{4,3,2,1,0:T(8,128)(2,1)S(1)}, u32[]{:S(2)}, u32[]{:S(2)}) collective-permute-start(bf16[2,2,3,256,128]{4,3,2,1,0:T(8,128)(2,1)} %slice.3), channel_id=1, source_target_pairs={{0,12},{4,0},{8,4},{12,8},{1,13},{5,1},{9,5},{13,9},{2,14},{6,2},{... | collective-permute-start | bytes 2359304 | tf_op jit(solution)/shard_map/ppermute | solution.py:487
  7.8 0.0 copy-start.5
  7.8 0.0 copy-start.6
  7.9 0.0 copy-start.1
  7.9 1.5 %copy.29 = f32[2,3,2,3,3,2048]{5,0,4,3,2,1:T(2,128)S(1)} copy(bf16[2,3,2,3,3,2048]{5,2,4,3,1,0:T(2,128)(2,1)} %param.7) | data formatting | bytes 1327104 | tf_op jit(solution)/shard_map/reshape | solution.py:509
  9.4 0.0 copy-done.2
  9.4 1.2 %copy.31.links_ref = bf16[2,3,2,3,3,2048]{5,4,3,2,1,0:T(4,128)(2,1)} copy(bf16[2,3,2,3,3,2048]{5,2,4,3,1,0:T(2,128)(2,1)S(1)} %copy-done.2) | data formatting | bytes 884736 | tf_op args[1]
  10.6 0.5 copy.30.links_ref
  11.1 0.5 compare_select_fusion.signs
  11.7 0.0 copy-done.5
  11.7 0.1 copy.32
  11.8 0.0 copy-done.6
  11.8 0.1 copy.36
  11.9 0.6 fusion.5.positions
  12.5 0.0 copy-done.1
  12.5 37.5 %local_gram.1.part_ref = f32[2,2,128,256]{3,2,1,0:T(8,128)S(1)} custom-call(s32[2]{0:T(128)S(1)} %copy-done.1, f32[2,8]{1,0:T(2,128)S(1)} %pad_maximum_fusion.phases, bf16[2,2,3,2048,128]{4,3,2,1,0:T(8,128)(2,1)} %v_ref.3, f32[2,3,18,2048]{3,2,1,0:T(8,128)S(1)} %copy.30.links_ref), custom_call_target="tpu_custom_call" | custom-call | flops 12999999488 | bytes 6291456 | tf_op jit(solution)/shard_map/local_gram/pallas_call | solution.py:511
  49.9 0.0 copy-start
  49.9 0.8 copy-done
  50.7 0.0 collective-permute-done.above_ref
  50.7 0.0 copy-start.3
  50.7 0.9 copy-done.3
  51.6 4.8 %boundary.1.in_ref = f32[4,2,2,32,256]{4,3,2,1,0:T(8,128)} custom-call(s32[2]{0:T(128)} %dirs.3, bf16[2,2,3,2048,128]{4,3,2,1,0:T(8,128)(2,1)} %v_ref.3, bf16[2,3,2,3,3,2048]{5,4,3,2,1,0:T(4,128)(2,1)} %copy.31.links_ref, bf16[2,2,3,256,128]{4,3,2,1,0:T(8,128)(2,1)} %copy-done.3, f32[2,2,128,256]{3,2,1,0:T(8,128)} %copy-done), custom_call_target="tpu_custom_call" | custom-call | tf_op jit(solution)/shard_map/boundary/pallas_call | solution.py:539
  56.4 10.5 %reduce_rows.1 = (f32[2,2,32,256]{3,2,1,0:T(8,128)}, bf16[2,2,32,256]{3,2,1,0:T(8,128)(2,1)}) custom-call(f32[4,2,2,32,256]{4,3,2,1,0:T(8,128)} %boundary.1.in_ref), custom_call_target="tpu_custom_call" | custom-call | tf_op jit(solution)/shard_map/reduce_rows/pallas_call | solution.py:388
  66.9 15.5 %gather_all.1 = bf16[4,2,2,2,2,32,256]{6,5,4,3,2,1,0:T(8,128)(2,1)} custom-call(bf16[2,2,32,256]{3,2,1,0:T(8,128)(2,1)} %get-tuple-element.5.in_ref), custom_call_target="tpu_custom_call" | custom-call | tf_op jit(solution)/shard_map/gather_all/pallas_call | solution.py:467
  82.4 0.0 copy-start.4
  82.4 5.5 %contract.1 = f32[4,2,8,128]{3,2,1,0:T(8,128)} custom-call(s32[4,2]{1,0:T(4,128)} %fusion.5.positions, f32[8]{0:T(128)} %compare_select_fusion.signs, bf16[4,16,32,256]{3,2,1,0:T(8,128)(2,1)} %bitcast.4, bf16[4,16,32,256]{3,2,1,0:T(8,128)(2,1)} %bitcast.5, bf16[4,8,2,128,128]{4,3,2,1,0:T(8,128)(2,1)} %tau_ref.1), custom_call_target="tpu_custom_call" | custom-call | tf_op jit(solution)/shard_map/contract/pallas_call | solution.py:570
  88.0 0.9 reduce_sum.9
  88.8 0.4 collective-permute-start.1
  89.2 0.0 copy-done.4
  89.2 0.7 reshape.37
  90.0 0.1 collective-permute-done.1
  90.1 0.7 copy.40
  (4 shorter events, 0.1 us)
Async XLA Ops:
  0.6 8.8 %copy-start.2 = (bf16[2,3,2,3,3,2048]{5,2,4,3,1,0:T(2,128)(2,1)S(1)}, bf16[2,3,2,3,3,2048]{5,2,4,3,1,0:T(2,128)(2,1)}, u32[]{:S(2)}) copy-start(bf16[2,3,2,3,3,2048]{5,2,4,3,1,0:T(2,128)(2,1)} %param.7) | copy-start | bytes 1327108
  2.8 48.0 %collective-permute-start = (bf16[2,2,3,256,128]{4,3,2,1,0:T(8,128)(2,1)}, bf16[2,2,3,256,128]{4,3,2,1,0:T(8,128)(2,1)S(1)}, u32[]{:S(2)}, u32[]{:S(2)}) collective-permute-start(bf16[2,2,3,256,128]{4,3,2,1,0:T(8,128)(2,1)} %slice.3), channel_id=1, source_target_pairs={{0,12},{4,0},{8,4},{12,8},{1,13},{5,1},{9,5},{13,9},{2,14},{6,2},{... | collective-permute-start | bytes 2359304 | tf_op jit(solution)/shard_map/ppermute | solution.py:487
  7.8 3.8 %copy-start.5 = (s32[4,2]{0,1:T(2,128)S(1)}, s32[4,2]{0,1:T(2,128)}, u32[]{:S(2)}) copy-start(s32[4,2]{0,1:T(2,128)} %param.9) | copy-start | bytes 100
  7.8 3.9 %copy-start.6 = (s32[4,2]{0,1:T(2,128)S(1)}, s32[4,2]{0,1:T(2,128)}, u32[]{:S(2)}) copy-start(s32[4,2]{0,1:T(2,128)} %param.10) | copy-start | bytes 100
  7.9 4.6 %copy-start.1 = (s32[2]{0:T(128)S(1)}, s32[2]{0:T(128)}, u32[]{:S(2)}) copy-start(s32[2]{0:T(128)} %dirs.3) | copy-start | bytes 28
  49.9 0.8 copy-start
  50.7 0.9 copy-start.3
  82.4 6.8 %copy-start.4 = (f32[2,2,32,256]{3,2,1,0:T(8,128)S(1)}, f32[2,2,32,256]{3,2,1,0:T(8,128)}, u32[]{:S(2)}) copy-start(f32[2,2,32,256]{3,2,1,0:T(8,128)} %get-tuple-element.4) | copy-start | bytes 393220
  88.8 1.2 %collective-permute-start.1 = (f32[4,2]{1,0:T(4,128)S(1)}, f32[4,2]{1,0:T(4,128)S(1)}, u32[]{:S(2)}, u32[]{:S(2)}) collective-permute-start(f32[4,2]{1,0:T(4,128)S(1)} %broadcast_multiply_fusion), channel_id=1, source_target_pairs={{0,1},{1,0},{2,3},{3,2},{4,5},{5,4},{6,7},{7,6},{8,9},{9,8},{10,11... | collective-permute-start | bytes 104 | tf_op jit(solution)/shard_map/ppermute | solution.py:487

commit v5 on v4

--- a/solution.py
+++ b/solution.py
@@ -31,7 +31,7 @@
         parts = []
         for part in range(2):
             for a in range(3):
-                row = links_ref[lead + (part, a, pl.ds(b, 1), pl.ds(offset, group))]
+                row = links_ref[lead + (pl.ds(part * 9 + a * 3 + b, 1), pl.ds(offset, group))].astype(BF)
                 parts.append(jnp.broadcast_to(row, (group, group)) * mask)
         rows.append(jnp.concatenate(parts, axis=1))
     matrix = jnp.concatenate(rows, axis=0)
@@ -544,7 +544,7 @@
             grid=(slices,),
             in_specs=[
                 pl.BlockSpec((1, 2, 3, PLANE, columns), lambda t, d: (t, 0, 0, last, 0)),
-                pl.BlockSpec((1, 1, 2, 3, 3, PLANE), lambda t, d: (t, 2, 0, 0, 0, last)),
+                pl.BlockSpec((1, 1, 18, PLANE), lambda t, d: (t, 2, 0, last)),
                 pl.BlockSpec((1, 2, 3, PLANE, columns), lambda t, d: (t, 0, 0, 0, 0)),
                 pl.BlockSpec((1, op_slots, columns, 2 * columns), lambda t, d: (t, 0, 0, 0)),
             ],
@@ -553,7 +553,7 @@
             ),
         ),
         name="boundary",
-    )(directions, eigvecs, links, above, partial)
+    )(directions, eigvecs, flat, above, partial)
 
     elementals, halves = reduce_rows(summed, layers)
     elementals = elementals.reshape(slices, op_slots, rows, 2, columns)

time: 90.3 us -> 89.2 us (0.988)
  Pallas kernels: 73.8 us -> 72 us
  local copies, waits for them, and re-layouts: 8.59 us -> 7.43 us
    pallas_call x1, Pallas kernels: 15.5 us -> 30.4 us  [gather_all(): pl.pallas_call(functools.partial(gather_kernel, layers, times, cores), ou...]
    pallas_call x1, Pallas kernels: 37.5 us -> 22.8 us  [shards(): pl.pallas_call(functools.partial(local_kernel, plane_count, columns, scal...]
    pallas_call x1, Pallas kernels: 4.81 us -> 2.95 us  [shards(): pl.pallas_call(functools.partial(boundary_kernel, columns, scaling), out_...]
    unnamed x18 -> x15, local copies, waits for them, and re-layouts: 3.68 us -> 2.6 us
    slice x1, local copies, waits for them, and re-layouts: 2.13 us -> 1.19 us  [halo(): plane = eigvecs[:, :, :, :PLANE]]
    reshape x1, local copies, waits for them, and re-layouts: 0.72 us -> 1.62 us  [shards(): elementals = elementals.reshape(slices, op_slots, rows, 2, columns)]
  transfers between devices with their start and end apart: 2 -> 2, of which waited for: 1 -> 1; matrix products, arithmetic and copies ran while one was open for 6% -> 4% of each run, Pallas kernels for 41% -> 26%
where the time goes in v5:
time: 89.2 us; the launch traced here: 88.7 us
  Pallas kernels  72 us (81%)
  local copies, waits for them, and re-layouts  7.43 us (8%)
  starting transfers between devices  5.54 us (6%)
  other arithmetic  2.15 us (2%)
    pallas_call x1, Pallas kernels, gather_all(): pl.pallas_call(functools.partial(gather_kernel, layers, times, cores), ou...  30.4 us
    pallas_call x1, Pallas kernels, shards(): pl.pallas_call(functools.partial(local_kernel, plane_count, columns, scal...  22.8 us
    pallas_call x1, Pallas kernels, reduce_rows(): pl.pallas_call(functools.partial(reduce_kernel, layers), out_shape=(jax.S...  10.5 us
    ppermute x2, starting transfers between devices, shift_over(): lax.ppermute(array, axis, [(i, (i + by) % count) for i in range(count)])  5.54 us
    pallas_call x1, Pallas kernels, shards(): pl.pallas_call(functools.partial(contract_kernel, columns, 4), out_shape=...  5.41 us
    pallas_call x1, Pallas kernels, shards(): pl.pallas_call(functools.partial(boundary_kernel, columns, scaling), out_...  2.95 us
    unnamed x15, local copies, waits for them, and re-layouts  2.6 us
    reshape x2, local copies, waits for them, and re-layouts, shards(): flat = links.astype(F32).reshape(slices, 3, 18, local_sites)  2.02 us
  transfers between devices with their start and end apart: 2, of which 1 were waited for; matrix products, arithmetic and copies ran while one was open for 4% of the time, Pallas kernels for 26%

profile of v5, /device:TPU:0, one launch (start us, length us, event | category | flops | bytes accessed | tf_op | source)
XLA Modules:
  0.0 88.7 jit_solution(10806446981836082488)
XLA Ops:
  0.6 0.0 copy-start.4
  0.6 1.2 %slice.3 = bf16[2,2,3,256,128]{4,3,2,1,0:T(8,128)(2,1)S(1)} slice(bf16[2,2,3,2048,128]{4,3,2,1,0:T(8,128)(2,1)} %v_ref.3), slice={[0:2], [0:2], [0:3], [0:256], [0:128]} | slice | bytes 1572864 | tf_op jit(solution)/shard_map/slice | solution.py:491
  1.8 0.0 copy-start.5
  1.8 0.0 copy-start.2
  1.9 5.1 %collective-permute-start = (bf16[2,2,3,256,128]{4,3,2,1,0:T(8,128)(2,1)S(1)}, bf16[2,2,3,256,128]{4,3,2,1,0:T(8,128)(2,1)S(1)}, u32[]{:S(2)}, u32[]{:S(2)}) collective-permute-start(bf16[2,2,3,256,128]{4,3,2,1,0:T(8,128)(2,1)S(1)} %slice.3), channel_id=1, source_target_pairs={{0,12},{4,0},{8,4},{12,8},{1,13},{5,1},{9,5},{13,9},{2,14},{6,2},{... | collective-permute-start | bytes 2359304 | tf_op jit(solution)/shard_map/ppermute | solution.py:487
  7.0 1.5 %copy.28 = f32[2,3,2,3,3,2048]{5,0,4,3,2,1:T(2,128)S(1)} copy(bf16[2,3,2,3,3,2048]{5,2,4,3,1,0:T(2,128)(2,1)} %param.7) | data formatting | bytes 1327104 | tf_op jit(solution)/shard_map/reshape | solution.py:509
  8.5 0.5 copy.30.links_ref
  9.0 0.0 copy-start
  9.1 0.0 copy-done.4
  9.1 0.1 copy.31
  9.2 0.0 copy-done.5
  9.2 0.1 copy.35
  9.3 0.6 compare_select_fusion.signs
  9.9 0.6 fusion.5.positions
  10.5 0.0 copy-done.2
  10.5 22.8 %local_gram.1.part_ref = f32[2,2,128,256]{3,2,1,0:T(8,128)S(1)} custom-call(s32[2]{0:T(128)S(1)} %copy-done.2, f32[2,8]{1,0:T(2,128)S(1)} %pad_maximum_fusion.phases, bf16[2,2,3,2048,128]{4,3,2,1,0:T(8,128)(2,1)} %v_ref.3, f32[2,3,18,2048]{3,2,1,0:T(8,128)S(1)} %copy.30.links_ref), custom_call_target="tpu_custom_call" | custom-call | flops 12999999488 | bytes 6291456 | tf_op jit(solution)/shard_map/local_gram/pallas_call | solution.py:511
  33.3 0.0 copy-done
  33.4 0.0 copy-start.1
  33.4 0.8 copy-done.1
  34.2 0.0 collective-permute-done.above_ref
  34.2 0.0 copy-start.3
  34.2 0.9 %copy-done.3 = bf16[2,2,3,256,128]{4,3,2,1,0:T(8,128)(2,1)} copy-done((bf16[2,2,3,256,128]{4,3,2,1,0:T(8,128)(2,1)}, bf16[2,2,3,256,128]{4,3,2,1,0:T(8,128)(2,1)S(1)}, u32[]{:S(2)}) %copy-start.3) | copy-done | bytes 786456
  35.1 3.0 %boundary.1.in_ref = f32[4,2,2,32,256]{4,3,2,1,0:T(8,128)} custom-call(s32[2]{0:T(128)} %dirs.3, bf16[2,2,3,2048,128]{4,3,2,1,0:T(8,128)(2,1)} %v_ref.3, f32[2,3,18,2048]{3,2,1,0:T(8,128)} %copy-done, bf16[2,2,3,256,128]{4,3,2,1,0:T(8,128)(2,1)} %copy-done.3, f32[2,2,128,256]{3,2,1,0:T(8,128)} %copy-done.1), custom_call_target="tpu_custom_call" | custom-call | tf_op jit(solution)/shard_map/boundary/pallas_call | solution.py:539
  38.1 10.5 %reduce_rows.1 = (f32[2,2,32,256]{3,2,1,0:T(8,128)}, bf16[2,2,32,256]{3,2,1,0:T(8,128)(2,1)}) custom-call(f32[4,2,2,32,256]{4,3,2,1,0:T(8,128)} %boundary.1.in_ref), custom_call_target="tpu_custom_call" | custom-call | tf_op jit(solution)/shard_map/reduce_rows/pallas_call | solution.py:388
  48.6 1.6 %reshape.37 = f32[2,2,32,2,128]{4,3,2,1,0:T(2,128)} reshape(f32[2,2,32,256]{3,2,1,0:T(8,128)} %get-tuple-element.4) | data formatting | bytes 262144 | tf_op jit(solution)/shard_map/reshape | solution.py:559
  50.2 30.4 %gather_all.1 = bf16[4,2,2,2,2,32,256]{6,5,4,3,2,1,0:T(8,128)(2,1)} custom-call(bf16[2,2,32,256]{3,2,1,0:T(8,128)(2,1)} %get-tuple-element.5.in_ref), custom_call_target="tpu_custom_call" | custom-call | tf_op jit(solution)/shard_map/gather_all/pallas_call | solution.py:467
  80.6 5.4 %contract.1 = f32[4,2,8,128]{3,2,1,0:T(8,128)} custom-call(s32[4,2]{1,0:T(4,128)} %fusion.5.positions, f32[8]{0:T(128)} %compare_select_fusion.signs, bf16[4,16,32,256]{3,2,1,0:T(8,128)(2,1)} %bitcast.4, bf16[4,16,32,256]{3,2,1,0:T(8,128)(2,1)} %bitcast.5, bf16[4,8,2,128,128]{4,3,2,1,0:T(8,128)(2,1)} %tau_ref.1), custom_call_target="tpu_custom_call" | custom-call | tf_op jit(solution)/shard_map/contract/pallas_call | solution.py:570
  86.0 0.9 reduce_sum.9
  86.9 0.4 collective-permute-start.1
  87.3 0.8 collective-permute-done.1
  88.1 0.7 copy.39
  (4 shorter events, 0.1 us)
Async XLA Ops:
  0.6 8.5 %copy-start.4 = (s32[4,2]{0,1:T(2,128)S(1)}, s32[4,2]{0,1:T(2,128)}, u32[]{:S(2)}) copy-start(s32[4,2]{0,1:T(2,128)} %param.9) | copy-start | bytes 100
  1.8 7.4 %copy-start.5 = (s32[4,2]{0,1:T(2,128)S(1)}, s32[4,2]{0,1:T(2,128)}, u32[]{:S(2)}) copy-start(s32[4,2]{0,1:T(2,128)} %param.10) | copy-start | bytes 100
  1.8 8.7 %copy-start.2 = (s32[2]{0:T(128)S(1)}, s32[2]{0:T(128)}, u32[]{:S(2)}) copy-start(s32[2]{0:T(128)} %dirs.3) | copy-start | bytes 28
  1.9 32.3 %collective-permute-start = (bf16[2,2,3,256,128]{4,3,2,1,0:T(8,128)(2,1)S(1)}, bf16[2,2,3,256,128]{4,3,2,1,0:T(8,128)(2,1)S(1)}, u32[]{:S(2)}, u32[]{:S(2)}) collective-permute-start(bf16[2,2,3,256,128]{4,3,2,1,0:T(8,128)(2,1)S(1)} %slice.3), channel_id=1, source_target_pairs={{0,12},{4,0},{8,4},{12,8},{1,13},{5,1},{9,5},{13,9},{2,14},{6,2},{... | collective-permute-start | bytes 2359304 | tf_op jit(solution)/shard_map/ppermute | solution.py:487
  9.0 24.3 %copy-start = (f32[2,3,18,2048]{3,2,1,0:T(8,128)}, f32[2,3,18,2048]{3,2,1,0:T(8,128)S(1)}, u32[]{:S(2)}) copy-start(f32[2,3,18,2048]{3,2,1,0:T(8,128)S(1)} %copy.30.links_ref) | copy-start | bytes 2654212
  33.4 0.8 copy-start.1
  34.2 0.9 %copy-start.3 = (bf16[2,2,3,256,128]{4,3,2,1,0:T(8,128)(2,1)}, bf16[2,2,3,256,128]{4,3,2,1,0:T(8,128)(2,1)S(1)}, u32[]{:S(2)}) copy-start(bf16[2,2,3,256,128]{4,3,2,1,0:T(8,128)(2,1)S(1)} %collective-permute-done.above_ref) | copy-start | bytes 2359300
  86.9 1.2 %collective-permute-start.1 = (f32[4,2]{1,0:T(4,128)S(1)}, f32[4,2]{1,0:T(4,128)S(1)}, u32[]{:S(2)}, u32[]{:S(2)}) collective-permute-start(f32[4,2]{1,0:T(4,128)S(1)} %broadcast_multiply_fusion), channel_id=1, source_target_pairs={{0,1},{1,0},{2,3},{3,2},{4,5},{5,4},{6,7},{7,6},{8,9},{9,8},{10,11... | collective-permute-start | bytes 104 | tf_op jit(solution)/shard_map/ppermute | solution.py:487
